TPU v7x, 512 devices: a whole 4x4x16 slice. The times are simulated.
512 devices in a mesh: rows: 16 (over z_lo, x), cols: 32 (over y, z_hi, core).
Axes of the slice: x: 4, y: 4, z: 16 (z_hi: 4, z_lo: 4; z = z_hi * 4 + z_lo), core: 2. Of those that a mesh axis runs over, the one named last changes fastest.
Arguments:
- file_pixels: bfloat16 [48, 512, 4096], P(None, ('rows', 'cols')), may hold values from -6 to 6
- patchify_weight: bfloat16 [64, 48], replicated, may hold values from -0.875 to 0.875
- patchify_bias: float32 [64], replicated, may hold values from -3 to 3
- norm_gain: float32 [64], replicated, may hold values from 0.5 to 1.5
- norm_offset_vector: float32 [64], replicated, may hold values from -3 to 3
- kernel: float32 [64, 49], replicated, may hold values from -0.875 to 0.875
- kernel_offset: float32 [64], replicated, may hold values from -3 to 3
- cotangent: bfloat16 [64, 512, 4096], P(None, 'rows', 'cols'), may hold values from -10 to 10, as said below
Outputs:
- stem_output: bfloat16 [64, 512, 4096], P(None, 'rows', 'cols')
- weight_grad: float32 [64, 48], replicated
- bias_grad: float32 [64], replicated
- norm_scale_gradient: float32 [64], replicated
- shift_grad: float32 [64], replicated
- kernel_grad: float32 [64, 49], replicated
- offset_grad: float32 [64], replicated
Inputs may be any that keep to these rules, and one draw needn't show every extreme that they name: A cotangent of order one.
All inputs are finite; a program needn't handle non-finite values.
Results may differ from a plain program's by a relative error of at most 0.0055.
Values may be sent and summed in bfloat16 or wider, within the bound.
A program may use at most 64 MiB of HBM per device.

v0:
```python
import math

import jax
import jax.numpy as jnp
from jax import lax
from jax.sharding import PartitionSpec as P

norm_eps = 1e-06
side = 7


def extended(block, sides, width):
    for axis, dim in sides:
        count = lax.axis_size(axis)
        forward = [(i, i + 1) for i in range(count - 1)]
        backward = [(target, source) for source, target in forward]
        low = lax.ppermute(
            lax.slice_in_dim(block, block.shape[dim] - width, None, axis=dim), axis, forward
        )
        high = lax.ppermute(lax.slice_in_dim(block, 0, width, axis=dim), axis, backward)
        block = jnp.concatenate([low, block, high], axis=dim)
    return block


def embed_patches(pixel_values, weight, bias):
    flat = pixel_values.reshape(pixel_values.shape[0], -1)
    mixed = jnp.dot(weight, flat, preferred_element_type=jnp.float32) + bias[:, None]
    return mixed.astype(jnp.bfloat16).reshape(
        weight.shape[0], pixel_values.shape[1], pixel_values.shape[2]
    )


def apply_layer_norm(patch_embedding):
    values = patch_embedding.astype(jnp.float32)
    center = values - jnp.mean(values, axis=0, keepdims=True)
    spread = jnp.mean(center * center, axis=0, keepdims=True)
    inverse_deviation = lax.rsqrt(spread + norm_eps)
    return (center * inverse_deviation, inverse_deviation)


def depthwise(padded, taps, height, breadth):
    total = jnp.zeros((padded.shape[0], height, breadth), jnp.float32)
    for tap_row in range(side):
        for tap_col in range(side):
            window = padded[:, tap_row : tap_row + height, tap_col : tap_col + breadth].astype(
                jnp.float32
            )
            total = total + taps[:, tap_row * side + tap_col][:, None, None] * window
    return total


def kernel_terms(padded, upstream, height, breadth):
    terms = []
    for tap_row in range(side):
        for tap_col in range(side):
            window = padded[:, tap_row : tap_row + height, tap_col : tap_col + breadth].astype(
                jnp.float32
            )
            terms.append(jnp.sum(window * upstream, axis=(1, 2)))
    return jnp.stack(terms, axis=1)


def per_device(
    file_pixels,
    patchify_weight,
    patchify_bias,
    norm_gain,
    norm_offset_vector,
    kernel,
    kernel_offset,
    cotangent,
):
    height = cotangent.shape[1]
    breadth = cotangent.shape[2]
    factor = 1.0 / math.sqrt(height * lax.axis_size("rows") * breadth * lax.axis_size("cols"))
    patch_embedding = lax.all_to_all(
        embed_patches(file_pixels, patchify_weight, patchify_bias),
        "cols",
        split_axis=2,
        concat_axis=1,
        tiled=True,
    )
    centered_input, inverse_deviation = apply_layer_norm(patch_embedding)
    scale_factor = norm_gain[:, None, None]
    normalized_output = (centered_input * scale_factor + norm_offset_vector[:, None, None]).astype(
        jnp.bfloat16
    )
    tall = extended(normalized_output, (("rows", 1),), 3)
    padded = extended(tall, (("cols", 2),), 3)
    cot_tall = extended(cotangent, (("rows", 1),), 3)
    cot_pad = extended(cot_tall, (("cols", 2),), 3)
    stem_output = (
        depthwise(padded, kernel, height, breadth) + kernel_offset[:, None, None]
    ).astype(jnp.bfloat16)
    upstream = cotangent.astype(jnp.float32) * factor
    kernel_grad = kernel_terms(padded, upstream, height, breadth)
    offset_grad = jnp.sum(upstream, axis=(1, 2))
    normalized_gradient = depthwise(cot_pad, kernel[:, ::-1], height, breadth) * factor
    norm_scale_gradient = jnp.sum(normalized_gradient * centered_input, axis=(1, 2))
    shift_grad = jnp.sum(normalized_gradient, axis=(1, 2))
    input_gradient = normalized_gradient * scale_factor
    patch_gradient = inverse_deviation * (
        input_gradient
        - jnp.mean(input_gradient, axis=0, keepdims=True)
        - centered_input * jnp.mean(input_gradient * centered_input, axis=0, keepdims=True)
    )
    patch_gradient = patch_gradient.astype(jnp.bfloat16)
    local_grad = lax.all_to_all(patch_gradient, "cols", split_axis=1, concat_axis=2, tiled=True)
    partial_weight = lax.dot_general(
        local_grad.reshape(local_grad.shape[0], -1),
        file_pixels.reshape(file_pixels.shape[0], -1),
        (((1,), (1,)), ((), ())),
        preferred_element_type=jnp.float32,
    )
    bias_part = jnp.sum(local_grad.astype(jnp.float32), axis=(1, 2))
    totals = lax.psum(
        (partial_weight, bias_part, norm_scale_gradient, shift_grad, kernel_grad, offset_grad),
        ("rows", "cols"),
    )
    return (stem_output, totals[0], totals[1], totals[2], totals[3], totals[4], totals[5])


def solution(mesh):
    return jax.shard_map(
        per_device,
        mesh=mesh,
        in_specs=(
            P(None, ("rows", "cols"), None),
            P(),
            P(),
            P(),
            P(),
            P(),
            P(),
            P(None, "rows", "cols"),
        ),
        out_specs=(P(None, "rows", "cols"), P(), P(), P(), P(), P(), P()),
        check_vma=False,
    )
```

profile of v0, /device:TPU:1, one launch (start us, length us, event | category | flops | bytes accessed | tf_op | source)
XLA Modules:
  0.0 420.4 jit_solution(11450217107587844098)
XLA Ops:
  0.6 0.0 copy-start
  0.6 1.0 copy-done
  1.6 1.0 fusion.1
  2.7 2.8 copy.94
  5.5 0.5 broadcast.111
  6.0 22.4 %reduce.3 = bf16[4096,64]{1,0:T(8,128)(2,1)S(1)} reduce(bf16[4096,1,64]{2,1,0:T(2,128)(2,1)S(1)} %bitcast.174, bf16[]{:T(256)} %broadcast.111), dimensions={1}, to_apply=%bitcast.163.reduce_sub_computation | reduce | bytes 1048578
  28.4 1.5 reshape.173
  29.9 19.6 %all-to-all-start = ((bf16[32,2,4096]{2,1,0:T(2,128)(2,1)}), bf16[32,2,4096]{2,1,0:T(2,128)(2,1)}, u32[]{:S(2)}, u32[]{:S(2)}) async-start(bf16[32,2,4096]{2,1,0:T(2,128)(2,1)} %reshape.173), calls=%async_computation | async-start | bytes 1048576 | tf_op jit(solution)/shard_map/all_to_all | solution.py:76
  49.5 1.7 copy.98
  51.2 0.1 fusion.190
  51.4 3.1 collective-permute-start.4
  54.5 1.3 collective-permute-start.5
  55.8 0.5 slice_bitcast_fusion.48
  56.3 0.7 slice_bitcast_fusion.47
  57.0 0.6 slice_bitcast_fusion.46
  57.6 3.3 collective-permute-done.5
  61.0 8.4 %collective-permute-start.6 = (bf16[64,38,3]{0,1,2:T(8,128)(2,1)S(1)}, bf16[64,38,3]{0,1,2:T(8,128)(2,1)S(1)}, u32[]{:S(2)}, u32[]{:S(2)}) collective-permute-start(bf16[64,38,3]{0,1,2:T(8,128)(2,1)S(1)} %get-tuple-element.117), channel_id=1, source_target_pairs={{0,1},{1,2},{2,3},{3,4},{4,5},{5,6},{6,7},{7,8},{8,9},{9,10},{10,1... | collective-permute-start | bytes 43784 | tf_op jit(solution)/shard_map/ppermute | solution.py:17
  69.4 13.0 %collective-permute-start.7 = (bf16[64,38,3]{0,1,2:T(8,128)(2,1)S(1)}, bf16[64,38,3]{0,1,2:T(8,128)(2,1)S(1)}, u32[]{:S(2)}, u32[]{:S(2)}) collective-permute-start(bf16[64,38,3]{0,1,2:T(8,128)(2,1)S(1)} %get-tuple-element.118), channel_id=1, source_target_pairs={{1,0},{2,1},{3,2},{4,3},{5,4},{6,5},{7,6},{8,7},{9,8},{10,9},{11,1... | collective-permute-start | bytes 43784 | tf_op jit(solution)/shard_map/ppermute | solution.py:20
  82.4 0.5 broadcast_multiply_fusion.3
  83.0 3.8 maximum_maximum_fusion.1
  86.8 5.5 %reshape.174 = bf16[4096,1,64]{2,1,0:T(2,128)(2,1)} reshape(bf16[32,2,4096]{2,1,0:T(2,128)(2,1)} %all-to-all-done) | data formatting | bytes 1048576
  92.3 31.6 %convert_reduce_fusion.1 = f32[4096]{0:T(1024)S(1)} fusion(bf16[4096,1,64]{2,1,0:T(2,128)(2,1)} %reshape.174), kind=kLoop, calls=%fused_computation.334 | loop fusion | flops 520192 | bytes 540672 | tf_op jit(solution)/shard_map/reduce_sum | solution.py:35
  124.0 3.3 bitcast_convert_fusion
  127.2 58.9 %multiply_reduce_fusion.2 = f32[4096]{0:T(1024)S(1)} fusion(f32[4096]{0:T(1024)S(1)} %get-tuple-element.177, bf16[4096,1,64]{2,1,0:T(2,128)(2,1)S(1)} %copy-done.3), kind=kLoop, calls=%fused_computation.233 | loop fusion | flops 1044480 | bytes 557056 | tf_op jit(solution)/shard_map/reduce_sum | solution.py:36
  186.1 0.1 copy.97
  186.2 0.1 copy.95
  186.4 22.9 %multiply_reduce_fusion = (f32[64]{0:T(128)}, f32[32,128]{0,1:T(8,128)S(1)}, f32[32,128]{0,1:T(8,128)S(1)}, f32[64]{0:T(128)}, f32[64,32,128]{0,1,2:T(8,128)S(1)}) fusion(f32[32,128]{0,1:T(8,128)S(1)} %copy.97, f32[32,128]{0,1:T(8,128)S(1)} %copy.95, f32[64,32,128]{0,2,1:T(8,128)} %bitcast.172, f32[64]{0:T(128)} %broadcast_multiply_fusion.3, ...), kind=kLoop, calls=%fused_computation.228 | loop fusion | flops 45604736 | bytes 24818688 | tf_op jit(solution)/shard_map/reduce_sum | solution.py:99
  209.3 3.5 multiply_convert_fusion
  212.8 0.1 fusion.191
  212.9 3.1 collective-permute-start
  216.1 1.3 collective-permute-start.1
  217.4 0.6 collective-permute-done
  218.0 3.8 collective-permute-done.1
  221.8 9.0 %collective-permute-start.2 = (bf16[64,38,3]{0,1,2:T(8,128)(2,1)S(1)}, bf16[64,38,3]{0,1,2:T(8,128)(2,1)S(1)}, u32[]{:S(2)}, u32[]{:S(2)}) collective-permute-start(bf16[64,38,3]{0,1,2:T(8,128)(2,1)S(1)} %get-tuple-element.121), channel_id=1, source_target_pairs={{0,1},{1,2},{2,3},{3,4},{4,5},{5,6},{6,7},{7,8},{8,9},{9,10},{10,1... | collective-permute-start | bytes 43784 | tf_op jit(solution)/shard_map/ppermute | solution.py:17
  230.8 1.9 collective-permute-start.3
  232.7 1.9 copy.104
  234.6 14.7 %all-to-all-start.1 = ((bf16[64,32,128]{2,0,1:T(8,128)(2,1)}), bf16[64,32,128]{2,0,1:T(8,128)(2,1)S(1)}, u32[]{:S(2)}, u32[]{:S(2)}) async-start(bf16[64,32,128]{2,0,1:T(8,128)(2,1)} %copy.104), calls=%async_computation.1 | async-start | bytes 1048576 | tf_op jit(solution)/shard_map/all_to_all | solution.py:108
  249.4 4.1 maximum_maximum_fusion
  253.9 7.2 %fusion.148 = (f32[64]{0:T(128)}, f32[64]{0:T(128)}, f32[64]{0:T(128)}, f32[64]{0:T(128)}, f32[64]{0:T(128)}, /*index=5*/f32[64]{0:T(128)}, f32[64]{0:T(128)}, f...) fusion(bf16[64,32,128]{0,1,2:T(8,128)(2,1)S(1)} %copy-done.2, ...), kind=kLoop, calls=%fused_computation.200 | loop fusion | flops 14678912 | bytes 9966080 | tf_op jit(solution)/shard_map/reduce_sum | solution.py:59
  261.5 17.8 %add_convert_fusion = bf16[64,32,128]{0,1,2:T(8,128)(2,1)} fusion(bf16[64,32,128]{0,1,2:T(8,128)(2,1)S(1)} %copy-done.5, bf16[64,3,128]{0,1,2:T(4,128)(2,1)S(1)} %copy-done.8, bf16[64,3,128]{0,1,2:T(4,128)(2,1)S(1)} %collective-permute-done, f32[64]{0:T(128)} %param.14, f32[64]{0:T(128)S(1)} %copy-done.50, f32[64]{0:T(128)S(1)} %copy-done.51, ...), kind=kLoop, calls=%fused_computation.231 | loop fusion | flops 43515904 | bytes 23179776 | tf_op jit(solution)/shard_map/convert_element_type | solution.py:94
  279.3 4.6 %fusion.147 = (f32[64]{0:T(128)S(1)}, f32[64]{0:T(128)S(1)}, f32[64]{0:T(128)S(1)}, f32[64]{0:T(128)S(1)}, f32[64]{0:T(128)S(1)}, /*index=5*/f32[64]{0:T(128)S(1...) fusion(bf16[64,32,128]{0,1,2:T(8,128)(2,1)S(1)} %copy-done.2, ...), kind=kLoop, calls=%fused_computation.199 | loop fusion | flops 13106560 | bytes 2722304 | tf_op jit(solution)/shard_map/reduce_sum | solution.py:59
  283.9 3.6 copy.106
  287.5 0.8 fusion.102
  288.5 6.8 %fusion.144 = (f32[64]{0:T(128)S(1)}, f32[64]{0:T(128)S(1)}, f32[64]{0:T(128)S(1)}, f32[64]{0:T(128)S(1)}, f32[64]{0:T(128)S(1)}, /*index=5*/f32[64]{0:T(128)S(1...) fusion(bf16[64,32,128]{0,1,2:T(8,128)(2,1)S(1)} %copy-done.2, ...), kind=kLoop, calls=%fused_computation.196 | loop fusion | flops 14940992 | bytes 9966336 | tf_op jit(solution)/shard_map/reduce_sum | solution.py:59
  295.5 0.1 stack.199
  295.7 0.2 convert_reduce_fusion
  295.8 0.3 fusion.183
  296.1 123.9 %all-reduce = (f32[64,48]{0,1:T(8,128)}, f32[64]{0:T(128)}, f32[64]{0:T(128)}, f32[64]{0:T(128)}, f32[64,49]{0,1:T(8,128)}, /*index=5*/f32[64]{0:T(128)}) all-reduce(f32[64,48]{0,1:T(8,128)S(1)} %fusion.183, f32[64]{0:T(128)S(1)} %convert_reduce_fusion, f32[64]{0:T(128)S(1)} %copy-done.70, ...), channel_id=1, replica_groups=mesh['rows'=16,'cols'=32] {'rows','cols'}, use_global_device_ids=true, to_apply=%region_4.0 | all-reduce | flops 6464 | bytes 51712 | tf_op jit(solution)/shard_map/psum | solution.py:116
  (162 shorter events, 0.4 us)
Async XLA Ops:
  28.4 21.1 %copy-start.9 = (bf16[64,32,128]{2,1,0:T(8,128)(2,1)S(1)}, bf16[64,32,128]{2,1,0:T(8,128)(2,1)}, u32[]{:S(2)}) copy-start(bf16[64,32,128]{2,1,0:T(8,128)(2,1)} %param.15) | copy-start | bytes 1572868
  28.4 27.4 %copy-start.10 = (f32[64,49]{0,1:T(8,128)S(1)}, f32[64,49]{0,1:T(8,128)}, u32[]{:S(2)}) copy-start(f32[64,49]{0,1:T(8,128)} %param.13) | copy-start | bytes 37636
  29.9 52.5 %copy-start.73 = (f32[64]{0:T(128)S(1)}, f32[64]{0:T(128)}, u32[]{:S(2)}) copy-start(f32[64]{0:T(128)} %param.11) | copy-start | bytes 772
  29.9 56.8 %all-to-all-start = ((bf16[32,2,4096]{2,1,0:T(2,128)(2,1)}), bf16[32,2,4096]{2,1,0:T(2,128)(2,1)}, u32[]{:S(2)}, u32[]{:S(2)}) async-start(bf16[32,2,4096]{2,1,0:T(2,128)(2,1)} %reshape.173), calls=%async_computation | async-start | bytes 1048576 | tf_op jit(solution)/shard_map/all_to_all | solution.py:76
  51.2 31.7 %copy-start.1 = (bf16[64,32,128]{0,1,2:T(8,128)(2,1)}, bf16[64,32,128]{0,1,2:T(8,128)(2,1)S(1)}, u32[]{:S(2)}) copy-start(bf16[64,32,128]{0,1,2:T(8,128)(2,1)S(1)} %copy.98) | copy-start | bytes 1572868
  51.4 6.3 %collective-permute-start.4 = (bf16[64,3,128]{0,1,2:T(4,128)(2,1)S(1)}, bf16[64,3,128]{0,1,2:T(4,128)(2,1)S(1)}, u32[]{:S(2)}, u32[]{:S(2)}) collective-permute-start(bf16[64,3,128]{0,1,2:T(4,128)(2,1)S(1)} %get-tuple-element.123), channel_id=1, source_target_pairs={{0,32},{32,64},{64,96},{96,128},{128,160},{160,192},{192,224},{224... | collective-permute-start | bytes 147464 | tf_op jit(solution)/shard_map/ppermute | solution.py:17
  54.5 6.5 %collective-permute-start.5 = (bf16[64,3,128]{0,1,2:T(4,128)(2,1)S(1)}, bf16[64,3,128]{0,1,2:T(4,128)(2,1)S(1)}, u32[]{:S(2)}, u32[]{:S(2)}) collective-permute-start(bf16[64,3,128]{0,1,2:T(4,128)(2,1)S(1)} %get-tuple-element.124), channel_id=1, source_target_pairs={{32,0},{64,32},{96,64},{128,96},{160,128},{192,160},{224,192},{256... | collective-permute-start | bytes 147464 | tf_op jit(solution)/shard_map/ppermute | solution.py:20
  56.3 130.0 %copy-start.11 = (f32[64]{0:T(128)}, f32[64]{0:T(128)S(1)}, u32[]{:S(2)}) copy-start(f32[64]{0:T(128)S(1)} %get-tuple-element.139) | copy-start | bytes 772
  56.3 130.0 %copy-start.13 = (f32[64]{0:T(128)}, f32[64]{0:T(128)S(1)}, u32[]{:S(2)}) copy-start(f32[64]{0:T(128)S(1)} %get-tuple-element.140) | copy-start | bytes 772
  56.3 130.0 %copy-start.15 = (f32[64]{0:T(128)}, f32[64]{0:T(128)S(1)}, u32[]{:S(2)}) copy-start(f32[64]{0:T(128)S(1)} %get-tuple-element.141) | copy-start | bytes 772
  56.3 130.0 %copy-start.17 = (f32[64]{0:T(128)}, f32[64]{0:T(128)S(1)}, u32[]{:S(2)}) copy-start(f32[64]{0:T(128)S(1)} %get-tuple-element.142) | copy-start | bytes 772
  61.0 22.0 %collective-permute-start.6 = (bf16[64,38,3]{0,1,2:T(8,128)(2,1)S(1)}, bf16[64,38,3]{0,1,2:T(8,128)(2,1)S(1)}, u32[]{:S(2)}, u32[]{:S(2)}) collective-permute-start(bf16[64,38,3]{0,1,2:T(8,128)(2,1)S(1)} %get-tuple-element.117), channel_id=1, source_target_pairs={{0,1},{1,2},{2,3},{3,4},{4,5},{5,6},{6,7},{7,8},{8,9},{9,10},{10,1... | collective-permute-start | bytes 43784 | tf_op jit(solution)/shard_map/ppermute | solution.py:17
  69.4 13.5 %collective-permute-start.7 = (bf16[64,38,3]{0,1,2:T(8,128)(2,1)S(1)}, bf16[64,38,3]{0,1,2:T(8,128)(2,1)S(1)}, u32[]{:S(2)}, u32[]{:S(2)}) collective-permute-start(bf16[64,38,3]{0,1,2:T(8,128)(2,1)S(1)} %get-tuple-element.118), channel_id=1, source_target_pairs={{1,0},{2,1},{3,2},{4,3},{5,4},{6,5},{7,6},{8,7},{9,8},{10,9},{11,1... | collective-permute-start | bytes 43784 | tf_op jit(solution)/shard_map/ppermute | solution.py:20
  92.3 31.7 %copy-start.3 = (bf16[4096,1,64]{2,1,0:T(2,128)(2,1)S(1)}, bf16[4096,1,64]{2,1,0:T(2,128)(2,1)}, u32[]{:S(2)}) copy-start(bf16[4096,1,64]{2,1,0:T(2,128)(2,1)} %reshape.174) | copy-start | bytes 1572868
  186.4 22.9 %copy-start.6 = (f32[64,1,4096]{0,1,2:T(1,128)S(1)}, f32[64,1,4096]{0,1,2:T(1,128)}, u32[]{:S(2)}) copy-start(f32[64,1,4096]{0,1,2:T(1,128)} %bitcast_convert_fusion) | copy-start | bytes 3145732
  186.4 22.9 %copy-start.72 = (f32[64]{0:T(128)S(1)}, f32[64]{0:T(128)}, u32[]{:S(2)}) copy-start(f32[64]{0:T(128)} %broadcast_multiply_fusion.3) | copy-start | bytes 772
  186.4 22.9 %copy-start.74 = (f32[64]{0:T(128)S(1)}, f32[64]{0:T(128)}, u32[]{:S(2)}) copy-start(f32[64]{0:T(128)} %param.11) | copy-start | bytes 772
  186.4 22.9 %copy-start.75 = (f32[64]{0:T(128)S(1)}, f32[64]{0:T(128)}, u32[]{:S(2)}) copy-start(f32[64]{0:T(128)} %param.12) | copy-start | bytes 772
  212.8 9.0 %copy-start.4 = (bf16[64,32,128]{0,1,2:T(8,128)(2,1)}, bf16[64,32,128]{0,1,2:T(8,128)(2,1)S(1)}, u32[]{:S(2)}) copy-start(bf16[64,32,128]{0,1,2:T(8,128)(2,1)S(1)} %get-tuple-element.114) | copy-start | bytes 1572868
  212.9 5.1 %collective-permute-start = (bf16[64,3,128]{0,1,2:T(4,128)(2,1)S(1)}, bf16[64,3,128]{0,1,2:T(4,128)(2,1)S(1)}, u32[]{:S(2)}, u32[]{:S(2)}) collective-permute-start(bf16[64,3,128]{0,1,2:T(4,128)(2,1)S(1)} %get-tuple-element.125), channel_id=1, source_target_pairs={{0,32},{32,64},{64,96},{96,128},{128,160},{160,192},{192,224},{224... | collective-permute-start | bytes 147464 | tf_op jit(solution)/shard_map/ppermute | solution.py:17
  216.1 5.7 %collective-permute-start.1 = (bf16[64,3,128]{0,1,2:T(4,128)(2,1)S(1)}, bf16[64,3,128]{0,1,2:T(4,128)(2,1)S(1)}, u32[]{:S(2)}, u32[]{:S(2)}) collective-permute-start(bf16[64,3,128]{0,1,2:T(4,128)(2,1)S(1)} %get-tuple-element.126), channel_id=1, source_target_pairs={{32,0},{64,32},{96,64},{128,96},{160,128},{192,160},{224,192},{256... | collective-permute-start | bytes 147464 | tf_op jit(solution)/shard_map/ppermute | solution.py:20
  221.8 27.6 %copy-start.7 = (bf16[64,3,128]{0,1,2:T(4,128)(2,1)}, bf16[64,3,128]{0,1,2:T(4,128)(2,1)S(1)}, u32[]{:S(2)}) copy-start(bf16[64,3,128]{0,1,2:T(4,128)(2,1)S(1)} %collective-permute-done.1) | copy-start | bytes 147460
  221.8 27.5 %collective-permute-start.2 = (bf16[64,38,3]{0,1,2:T(8,128)(2,1)S(1)}, bf16[64,38,3]{0,1,2:T(8,128)(2,1)S(1)}, u32[]{:S(2)}, u32[]{:S(2)}) collective-permute-start(bf16[64,38,3]{0,1,2:T(8,128)(2,1)S(1)} %get-tuple-element.121), channel_id=1, source_target_pairs={{0,1},{1,2},{2,3},{3,4},{4,5},{5,6},{6,7},{7,8},{8,9},{9,10},{10,1... | collective-permute-start | bytes 43784 | tf_op jit(solution)/shard_map/ppermute | solution.py:17
  230.8 18.6 %collective-permute-start.3 = (bf16[64,38,3]{0,1,2:T(8,128)(2,1)S(1)}, bf16[64,38,3]{0,1,2:T(8,128)(2,1)S(1)}, u32[]{:S(2)}, u32[]{:S(2)}) collective-permute-start(bf16[64,38,3]{0,1,2:T(8,128)(2,1)S(1)} %get-tuple-element.122), channel_id=1, source_target_pairs={{1,0},{2,1},{3,2},{4,3},{5,4},{6,5},{7,6},{8,7},{9,8},{10,9},{11,1... | collective-permute-start | bytes 43784 | tf_op jit(solution)/shard_map/ppermute | solution.py:20
  234.6 61.0 %all-to-all-start.1 = ((bf16[64,32,128]{2,0,1:T(8,128)(2,1)}), bf16[64,32,128]{2,0,1:T(8,128)(2,1)S(1)}, u32[]{:S(2)}, u32[]{:S(2)}) async-start(bf16[64,32,128]{2,0,1:T(8,128)(2,1)} %copy.104), calls=%async_computation.1 | async-start | bytes 1048576 | tf_op jit(solution)/shard_map/all_to_all | solution.py:108
  253.5 7.6 %copy-start.5 = (bf16[64,32,128]{0,1,2:T(8,128)(2,1)S(1)}, bf16[64,32,128]{0,1,2:T(8,128)(2,1)}, u32[]{:S(2)}) copy-start(bf16[64,32,128]{0,1,2:T(8,128)(2,1)} %copy-done.4) | copy-start | bytes 1572868
  253.5 7.6 %copy-start.8 = (bf16[64,3,128]{0,1,2:T(4,128)(2,1)S(1)}, bf16[64,3,128]{0,1,2:T(4,128)(2,1)}, u32[]{:S(2)}) copy-start(bf16[64,3,128]{0,1,2:T(4,128)(2,1)} %copy-done.7) | copy-start | bytes 147460
  253.5 7.6 %copy-start.12 = (f32[64]{0:T(128)S(1)}, f32[64]{0:T(128)}, u32[]{:S(2)}) copy-start(f32[64]{0:T(128)} %copy-done.11) | copy-start | bytes 772
  253.5 7.6 %copy-start.14 = (f32[64]{0:T(128)S(1)}, f32[64]{0:T(128)}, u32[]{:S(2)}) copy-start(f32[64]{0:T(128)} %copy-done.13) | copy-start | bytes 772
  253.5 7.6 %copy-start.16 = (f32[64]{0:T(128)S(1)}, f32[64]{0:T(128)}, u32[]{:S(2)}) copy-start(f32[64]{0:T(128)} %copy-done.15) | copy-start | bytes 772
  253.6 7.6 %copy-start.18 = (f32[64]{0:T(128)S(1)}, f32[64]{0:T(128)}, u32[]{:S(2)}) copy-start(f32[64]{0:T(128)} %copy-done.17) | copy-start | bytes 772
  253.6 7.6 %copy-start.19 = (f32[64]{0:T(128)S(1)}, f32[64]{0:T(128)}, u32[]{:S(2)}) copy-start(f32[64]{0:T(128)} %get-tuple-element.143) | copy-start | bytes 772
  253.6 7.6 %copy-start.20 = (f32[64]{0:T(128)S(1)}, f32[64]{0:T(128)}, u32[]{:S(2)}) copy-start(f32[64]{0:T(128)} %get-tuple-element.144) | copy-start | bytes 772
  253.6 7.6 %copy-start.21 = (f32[64]{0:T(128)S(1)}, f32[64]{0:T(128)}, u32[]{:S(2)}) copy-start(f32[64]{0:T(128)} %get-tuple-element.145) | copy-start | bytes 772
  253.6 7.6 %copy-start.22 = (f32[64]{0:T(128)S(1)}, f32[64]{0:T(128)}, u32[]{:S(2)}) copy-start(f32[64]{0:T(128)} %get-tuple-element.146) | copy-start | bytes 772
  253.6 7.6 %copy-start.23 = (f32[64]{0:T(128)S(1)}, f32[64]{0:T(128)}, u32[]{:S(2)}) copy-start(f32[64]{0:T(128)} %get-tuple-element.147) | copy-start | bytes 772
  253.6 7.6 %copy-start.24 = (f32[64]{0:T(128)S(1)}, f32[64]{0:T(128)}, u32[]{:S(2)}) copy-start(f32[64]{0:T(128)} %get-tuple-element.148) | copy-start | bytes 772
  253.6 7.6 %copy-start.25 = (f32[64]{0:T(128)S(1)}, f32[64]{0:T(128)}, u32[]{:S(2)}) copy-start(f32[64]{0:T(128)} %get-tuple-element.149) | copy-start | bytes 772
  253.6 7.6 %copy-start.26 = (f32[64]{0:T(128)S(1)}, f32[64]{0:T(128)}, u32[]{:S(2)}) copy-start(f32[64]{0:T(128)} %get-tuple-element.150) | copy-start | bytes 772
  253.7 7.6 %copy-start.27 = (f32[64]{0:T(128)S(1)}, f32[64]{0:T(128)}, u32[]{:S(2)}) copy-start(f32[64]{0:T(128)} %get-tuple-element.151) | copy-start | bytes 772
  253.7 7.6 %copy-start.28 = (f32[64]{0:T(128)S(1)}, f32[64]{0:T(128)}, u32[]{:S(2)}) copy-start(f32[64]{0:T(128)} %get-tuple-element.152) | copy-start | bytes 772
  253.7 7.6 %copy-start.29 = (f32[64]{0:T(128)S(1)}, f32[64]{0:T(128)}, u32[]{:S(2)}) copy-start(f32[64]{0:T(128)} %get-tuple-element.153) | copy-start | bytes 772
  253.7 7.6 %copy-start.30 = (f32[64]{0:T(128)S(1)}, f32[64]{0:T(128)}, u32[]{:S(2)}) copy-start(f32[64]{0:T(128)} %get-tuple-element.154) | copy-start | bytes 772
  253.7 7.6 %copy-start.31 = (f32[64]{0:T(128)S(1)}, f32[64]{0:T(128)}, u32[]{:S(2)}) copy-start(f32[64]{0:T(128)} %get-tuple-element.155) | copy-start | bytes 772
  253.7 7.6 %copy-start.32 = (f32[64]{0:T(128)S(1)}, f32[64]{0:T(128)}, u32[]{:S(2)}) copy-start(f32[64]{0:T(128)} %get-tuple-element.156) | copy-start | bytes 772
  253.7 7.6 %copy-start.33 = (f32[64]{0:T(128)S(1)}, f32[64]{0:T(128)}, u32[]{:S(2)}) copy-start(f32[64]{0:T(128)} %get-tuple-element.157) | copy-start | bytes 772
  288.5 7.6 %copy-start.70 = (f32[64]{0:T(128)S(1)}, f32[64]{0:T(128)}, u32[]{:S(2)}) copy-start(f32[64]{0:T(128)} %get-tuple-element.42) | copy-start | bytes 772
  288.5 7.6 %copy-start.71 = (f32[64]{0:T(128)S(1)}, f32[64]{0:T(128)}, u32[]{:S(2)}) copy-start(f32[64]{0:T(128)} %get-tuple-element.97) | copy-start | bytes 772
  (38 other events, 267.7 us)
where the time goes:
time: 428 us; the launch traced here: 420 us
  other arithmetic  188 us (44%)
  blocking collectives  124 us (29%)
  starting transfers between devices  75.4 us (18%)
  local copies, waits for them, and re-layouts  21.3 us (5%)
  waiting for transfers between devices  7.75 us (2%)
    psum x1, blocking collectives, per_device(): lax.psum((partial_weight, bias_part, norm_scale_gradient, shift_grad, ker...  124 us
    reduce_sum x1, other arithmetic, apply_layer_norm(): spread = jnp.mean(center * center, axis=0, keepdims=True)  58.9 us
    reduce_sum x1, other arithmetic, apply_layer_norm(): center = values - jnp.mean(values, axis=0, keepdims=True)  31.6 us
    ppermute x4, starting transfers between devices, extended(): lax.ppermute(lax.slice_in_dim(block, block.shape[dim] - width, None, axis...  23.7 us
    reduce_sum x1, other arithmetic, per_device(): jnp.sum(normalized_gradient * centered_input, axis=(1, 2))  22.9 us
    unnamed x1, other arithmetic  22.4 us
    all_to_all x1, starting transfers between devices, per_device(): lax.all_to_all(embed_patches(file_pixels, patchify_weight, patchify_bias)...  19.6 us
    reduce_sum x4, other arithmetic, kernel_terms(): terms.append(jnp.sum(window * upstream, axis=(1, 2)))  19.4 us
  transfers between devices with their start and end apart: 10, of which 3 were waited for; matrix products, arithmetic and copies ran while one was open for 13% of the time, Pallas kernels for 0%

commit v1 on v0

v1 whole, which is shorter than its diff:
```python
import functools
import math

import jax
import jax.numpy as jnp
from jax import lax
from jax.experimental import pallas as pl
from jax.experimental.pallas import tpu as pltpu
from jax.sharding import PartitionSpec as P

MESH = pl.DeviceIdType.MESH
F32 = jnp.float32
BF16 = jnp.bfloat16
norm_eps = 1e-06
side = 7
reach = 3
lanes = 128
sub = 8
PLACE = {"z_lo": 4, "x": 4, "y": 4, "z_hi": 4, "core": 2}


def body(
    place,
    pix,
    cot,
    weight,
    bias,
    gain,
    shift,
    kernel,
    koff,
    stem,
    total,
    pixb,
    up,
    uph,
    nor,
    norh,
    xhat,
    inv,
    ng,
    acc,
    taps,
    cols,
    pgb,
    sums,
    urow,
    upack,
    upeer,
    prow,
    ppack,
    ppeer,
    pay,
    rs,
    part,
    ex,
    part2,
    ey,
    part3,
    tot,
    a_send,
    a_recv,
    own_sem,
    u_send,
    u_recv,
    p_send,
    p_recv,
    r_send,
    r_recv,
    e_send,
    e_recv,
    z_send,
    z_recv,
    g_send,
    g_recv,
):
    nr = place["z_lo"] * place["x"]
    nc = place["y"] * place["z_hi"] * place["core"]
    height = cot.shape[0]
    ch = cot.shape[1]
    npix = pix.shape[0]
    tall = height + 2 * reach
    groups = ch // sub
    factor = 1.0 / math.sqrt(height * nr * lanes * nc)
    row = lax.axis_index("rows")
    col = lax.axis_index("cols")
    nx, ncore, nzl, ny, nzh = (place[k] for k in ("x", "core", "z_lo", "y", "z_hi"))
    x, zl = lax.rem(row, nx), row // nx
    core = lax.rem(col, ncore)
    zh = lax.rem(col // ncore, nzh)
    y = col // (ncore * nzh)
    lane8 = lax.broadcasted_iota(jnp.int32, (sub, lanes), 1)
    lane = lax.broadcasted_iota(jnp.int32, (ch, lanes), 1)
    lanep = lax.broadcasted_iota(jnp.int32, (npix, lanes), 1)

    def at_row(step):
        return lax.rem(row + step + nr, nr)

    def at_col(step):
        return lax.rem(col + step + nc, nc)

    n1, n2, n3 = nx * ncore, ny * nzl, nzh
    me1, me2, me3 = x * ncore + core, y * nzl + zl, zh

    def peer1(m):
        return (zl * nx + m // ncore, (col - core) + lax.rem(m, ncore))

    def peer2(m):
        return (lax.rem(m, nzl) * nx + x, (m // nzl) * (ncore * nzh) + lax.rem(col, ncore * nzh))

    def peer3(m):
        return (row, y * (ncore * nzh) + m * ncore + core)

    barrier = pltpu.get_barrier_semaphore()

    def greet(device):
        pl.semaphore_signal(barrier, inc=1, device_id=device, device_id_type=MESH)

    def greet_col(d, carry):
        greet((row, at_col(d)))
        return carry

    lax.fori_loop(1, nc, greet_col, 0)
    near = [(dr, dc) for dr in (-1, 1) for dc in (-1, 0, 1)]
    for dr, dc in near:
        greet((at_row(dr), at_col(dc)))

    def greet1(d, carry):
        greet(peer1(lax.rem(me1 + d, n1)))
        return carry

    def greet2(d, carry):
        greet(peer2(lax.rem(me2 + d, n2)))
        return carry

    lax.fori_loop(1, n1, greet1, 0)
    lax.fori_loop(1, n2, greet2, 0)

    def pack(load, mask_lane, shape):
        def step(h, both):
            left, right = both
            v = load(h)
            at = 3 * h
            left = jnp.where(
                (mask_lane >= at) & (mask_lane < at + 3), pltpu.roll(v, at, 1), left
            )
            right = jnp.where(
                (mask_lane >= 125 - at) & (mask_lane < 128 - at),
                pltpu.roll(v, lanes - at, 1),
                right,
            )
            return left, right

        zero = jnp.zeros(shape, F32)
        v = load(0)
        first = (
            jnp.where(mask_lane < 3, v, zero),
            jnp.where(mask_lane >= 125, v, zero),
        )
        return lax.fori_loop(1, height, step, first)

    def lift(h, carry):
        up[h + reach] = cot[h].astype(F32)
        return carry

    lax.fori_loop(0, height, lift, 0)
    left, right = pack(lambda h: up[h + reach], lane, (ch, lanes))
    upack[0] = left.astype(BF16)
    upack[1] = right.astype(BF16)

    pl.semaphore_wait(barrier, (nc - 1) + len(near) + (n1 - 1) + (n2 - 1))

    def halo_copies(rows_lo, rows_hi, packed, row_dst, pack_dst, send, recv):
        copies = [
            pltpu.make_async_remote_copy(
                src_ref=rows_lo,
                dst_ref=row_dst.at[1],
                send_sem=send.at[0],
                recv_sem=recv.at[1],
                device_id=(at_row(-1), col),
                device_id_type=MESH,
            ),
            pltpu.make_async_remote_copy(
                src_ref=rows_hi,
                dst_ref=row_dst.at[0],
                send_sem=send.at[1],
                recv_sem=recv.at[0],
                device_id=(at_row(1), col),
                device_id_type=MESH,
            ),
        ]
        for which, dc in ((0, -1), (1, 1)):
            for dr in (0, -1, 1):
                slot = (1 - which) * 3 + (1 - dr)
                copies.append(
                    pltpu.make_async_remote_copy(
                        src_ref=packed.at[which],
                        dst_ref=pack_dst.at[slot],
                        send_sem=send.at[2 + slot],
                        recv_sem=recv.at[2 + slot],
                        device_id=(at_row(dr), at_col(dc)),
                        device_id_type=MESH,
                    )
                )
        return copies

    u_copies = halo_copies(
        cot.at[0:reach], cot.at[height - reach : height], upack, urow, upeer, u_send, u_recv
    )
    for copy in u_copies:
        copy.start()

    def block(c):
        return pl.ds(pl.multiple_of(c * lanes, lanes), lanes)

    def send_pix(d):
        target = at_col(d)
        return pltpu.make_async_remote_copy(
            src_ref=pix.at[:, block(target)],
            dst_ref=pixb.at[0:npix, block(col)],
            send_sem=a_send.at[d],
            recv_sem=a_recv.at[col],
            device_id=(row, target),
            device_id_type=MESH,
        )

    def got_pix(d):
        source = at_col(d)
        return pltpu.make_async_remote_copy(
            src_ref=pix.at[:, block(col)],
            dst_ref=pixb.at[0:npix, block(source)],
            send_sem=a_send.at[d],
            recv_sem=a_recv.at[source],
            device_id=(row, source),
            device_id_type=MESH,
        )

    def start_pix(d, carry):
        send_pix(d).start()
        return carry

    lax.fori_loop(1, nc, start_pix, 0)
    own = pltpu.make_async_copy(pix.at[:, block(col)], pixb.at[0:npix, block(col)], own_sem)
    own.start()

    eye = lax.broadcasted_iota(jnp.int32, (ch, ch), 0) == lax.broadcasted_iota(
        jnp.int32, (ch, ch), 1
    )
    for at, ref in enumerate((bias, gain, shift, koff)):
        line = jnp.broadcast_to(ref[...], (ch, ch))
        column = jnp.sum(jnp.where(eye, line, 0.0), axis=1, keepdims=True)
        cols[at] = jnp.broadcast_to(column, (ch, lanes))
    for tap in range(side * side):
        taps[tap] = jnp.broadcast_to(kernel[:, tap : tap + 1], (ch, lanes))
    extra = pixb.shape[0] - npix
    wide = pixb.shape[1]
    pixb[npix:, :] = jnp.where(
        lax.broadcasted_iota(jnp.int32, (extra, wide), 0) == 0, 1.0, 0.0
    ).astype(BF16)

    def clear(h, carry):
        ng[h] = jnp.zeros((ch, lanes), F32)
        acc[h] = cols[3]
        return carry

    lax.fori_loop(0, height, clear, 0)

    top, bottom = row > 0, row < nr - 1
    west, east = col > 0, col < nc - 1

    def spread(peer, out, width):
        for at, (first, count, rows_ok) in enumerate(
            ((height - reach, reach, top), (0, height, None), (0, reach, bottom))
        ):
            keep_l = west if rows_ok is None else west & rows_ok
            keep_r = east if rows_ok is None else east & rows_ok
            lo = jnp.where(keep_l, peer(at), 0.0)
            hi = jnp.where(keep_r, peer(3 + at), 0.0)
            base = (0, reach, reach + height)[at]

            def one(k, carry, first=first, base=base, lo=lo, hi=hi):
                h = first + k
                out[base + k] = jnp.where(
                    lane < 64,
                    pltpu.roll(hi, lax.rem(lanes - 3 * h, lanes), 1),
                    pltpu.roll(lo, 3 * h, 1),
                )
                return carry

            lax.fori_loop(0, count, one, 0)

    for copy in u_copies:
        copy.wait_recv()
    for k in range(reach):
        up[k] = jnp.where(top, urow[0, k].astype(F32), 0.0)
        up[height + reach + k] = jnp.where(bottom, urow[1, k].astype(F32), 0.0)
    spread(lambda slot: upeer[slot].astype(F32), uph, ch)

    def sweep(src, halo, out, flip, kg):
        def one(step, carry):
            g, j = step // side, lax.rem(step, side)
            gs = pl.ds(pl.multiple_of(g * sub, sub), sub)
            s = reach - j
            mask = (lane8 >= lanes - s) | (lane8 < -s)
            amount = lax.rem(s + lanes, lanes)
            if flip:
                t = [taps[(side - 1 - i) * side + (side - 1 - j), gs] for i in range(side)]
            else:
                t = [taps[i * side + j, gs] for i in range(side)]
            sumk = [None] * side
            live = {}
            us = {}
            for a in range(tall):
                v = pltpu.roll(jnp.where(mask, halo[a, gs], src[a, gs]), amount, 1)
                if a < height:
                    live[a] = out[a, gs]
                    if kg:
                        us[a] = up[a + reach, gs]
                for i in range(side):
                    h = a - i
                    if 0 <= h < height:
                        live[h] = live[h] + t[i] * v
                        if kg:
                            term = us[h] * v
                            sumk[i] = term if sumk[i] is None else sumk[i] + term
                h = a - (side - 1)
                if h >= 0:
                    out[h, gs] = live.pop(h)
                    us.pop(h, None)
            if kg:
                line = pay[gs]
                for i in range(side):
                    line = jnp.where(
                        lane8 == 64 + i * side + j,
                        jnp.sum(sumk[i], axis=1, keepdims=True) * factor,
                        line,
                    )
                pay[gs] = line
            return carry

        lax.fori_loop(0, groups * side, one, 0)

    sweep(up, uph, ng, True, False)

    def wait_pix(d, carry):
        got_pix(d).wait_recv()
        return carry

    lax.fori_loop(1, nc, wait_pix, 0)
    own.wait()
    left, right = pack(lambda h: pixb[0:npix, block(h)].astype(F32), lanep, (npix, lanes))
    ppack[0] = left.astype(BF16)
    ppack[1] = right.astype(BF16)
    p_copies = halo_copies(
        pixb.at[0:npix, 0 : reach * lanes],
        pixb.at[0:npix, (height - reach) * lanes : height * lanes],
        ppack,
        prow,
        ppeer,
        p_send,
        p_recv,
    )
    for copy in p_copies:
        copy.start()

    def embed(pixels):
        patch = jnp.dot(weight[...], pixels, preferred_element_type=F32) + cols[0]
        v = patch.astype(BF16).astype(F32)
        center = v - jnp.mean(v, axis=0, keepdims=True)
        deviation = lax.rsqrt(jnp.mean(center * center, axis=0, keepdims=True) + norm_eps)
        return center * deviation, deviation

    def finish(hat):
        return (hat * cols[1] + cols[2]).astype(BF16).astype(F32)

    sums[...] = jnp.zeros_like(sums)

    def inner(h, carry):
        hat, deviation = embed(pixb[0:npix, block(h)])
        nor[h + reach] = finish(hat)
        grad = ng[h] * factor
        sums[0] += grad * hat
        sums[1] += grad
        sums[2] += up[h + reach]
        xgrad = grad * cols[1]
        mean1 = jnp.mean(xgrad, axis=0, keepdims=True)
        mean2 = jnp.mean(xgrad * hat, axis=0, keepdims=True)
        pgb[:, block(h)] = (deviation * (xgrad - mean1 - hat * mean2)).astype(BF16)
        return carry

    lax.fori_loop(0, height, inner, 0)
    grads = lax.dot_general(
        pgb[...], pixb[...], (((1,), (1,)), ((), ())), preferred_element_type=F32
    )
    pay[...] = jnp.zeros_like(pay)
    pay[:, 0 : pixb.shape[0]] = grads

    for copy in p_copies:
        copy.wait_recv()
    for k in range(reach):
        ks = slice(k * lanes, (k + 1) * lanes)
        nor[k] = jnp.where(top, finish(embed(prow[0, :, ks])[0]), 0.0)
        nor[height + reach + k] = jnp.where(bottom, finish(embed(prow[1, :, ks])[0]), 0.0)
    spread(lambda slot: finish(embed(ppeer[slot])[0]), norh, ch)

    sweep(nor, norh, acc, False, True)

    def close(h, carry):
        stem[h] = acc[h].astype(BF16)
        return carry

    lax.fori_loop(0, height, close, 0)
    last = pay[...]
    for at, scale in ((0, 1.0), (1, 1.0), (2, factor)):
        last = jnp.where(
            lane == 64 + side * side + at,
            jnp.sum(sums[at], axis=1, keepdims=True) * scale,
            last,
        )
    pay[...] = last

    share = ch // n1

    def rows_of(m):
        return pl.ds(pl.multiple_of(m * share, share), share)

    def copy1(d):
        m = lax.rem(me1 + d, n1)
        return pltpu.make_async_remote_copy(
            src_ref=pay.at[rows_of(m)],
            dst_ref=rs.at[me1],
            send_sem=r_send.at[d],
            recv_sem=r_recv.at[me1],
            device_id=peer1(m),
            device_id_type=MESH,
        )

    def got1(d):
        m = lax.rem(me1 + d, n1)
        return pltpu.make_async_remote_copy(
            src_ref=pay.at[rows_of(m)],
            dst_ref=rs.at[m],
            send_sem=r_send.at[d],
            recv_sem=r_recv.at[m],
            device_id=peer1(m),
            device_id_type=MESH,
        )

    def exchange(source, slots, me, n, peer, send, recv):
        def put(d):
            m = lax.rem(me + d, n)
            return pltpu.make_async_remote_copy(
                src_ref=source,
                dst_ref=slots.at[me],
                send_sem=send.at[d],
                recv_sem=recv.at[me],
                device_id=peer(m),
                device_id_type=MESH,
            )

        def got(d):
            m = lax.rem(me + d, n)
            return pltpu.make_async_remote_copy(
                src_ref=source,
                dst_ref=slots.at[m],
                send_sem=send.at[d],
                recv_sem=recv.at[m],
                device_id=peer(m),
                device_id_type=MESH,
            )

        def start(d, carry):
            put(d).start()
            return carry

        def arrive(d, carry):
            got(d).wait_recv()
            return carry

        def sent(d, carry):
            put(d).wait_send()
            return carry

        lax.fori_loop(1, n, start, 0)
        slots[me] = source[...]
        lax.fori_loop(1, n, arrive, 0)
        return lambda: lax.fori_loop(1, n, sent, 0)

    def start1(d, carry):
        copy1(d).start()
        return carry

    def arrive1(d, carry):
        got1(d).wait_recv()
        return carry

    def sent1(d, carry):
        copy1(d).wait_send()
        return carry

    lax.fori_loop(1, n1, start1, 0)
    rs[me1] = pay[rows_of(me1)]
    lax.fori_loop(1, n1, arrive1, 0)

    def sum_of(slots, n):
        whole = slots[0]
        for k in range(1, n):
            whole = whole + slots[k]
        return whole

    part[...] = sum_of(rs, n1)
    done2 = exchange(part, ex, me2, n2, peer2, e_send, e_recv)
    part2[...] = sum_of(ex, n2)
    done3 = exchange(part2, ey, me3, n3, peer3, z_send, z_recv)
    part3[...] = sum_of(ey, n3)
    done4 = exchange(part3, tot, me1, n1, peer1, g_send, g_recv)
    for k in range(n1):
        total[k * share : (k + 1) * share, :] = tot[k]

    def sent_pix(d, carry):
        send_pix(d).wait_send()
        return carry

    lax.fori_loop(1, nc, sent_pix, 0)
    for copy in u_copies + p_copies:
        copy.wait_send()
    lax.fori_loop(1, n1, sent1, 0)
    done2()
    done3()
    done4()


def per_device(
    place,
    file_pixels,
    patchify_weight,
    patchify_bias,
    norm_gain,
    norm_offset_vector,
    kernel,
    kernel_offset,
    cotangent,
):
    ch, height, breadth = cotangent.shape
    npix = file_pixels.shape[0]
    nc = place["y"] * place["z_hi"] * place["core"]
    n1, n2, n3 = place["x"] * place["core"], place["y"] * place["z_lo"], place["z_hi"]
    share = ch // n1
    wide = nc * lanes
    tall = height + 2 * reach
    plane = (ch, lanes)
    vmem = pl.BlockSpec(memory_space=pltpu.VMEM)
    dma = pltpu.SemaphoreType.DMA
    scratch = [
        pltpu.VMEM((64, wide), BF16),
        pltpu.VMEM((tall,) + plane, F32),
        pltpu.VMEM((tall,) + plane, F32),
        pltpu.VMEM((tall,) + plane, F32),
        pltpu.VMEM((tall,) + plane, F32),
        pltpu.VMEM((1,) + plane, F32),
        pltpu.VMEM((sub, lanes), F32),
        pltpu.VMEM((height,) + plane, F32),
        pltpu.VMEM((height,) + plane, F32),
        pltpu.VMEM((side * side,) + plane, F32),
        pltpu.VMEM((4,) + plane, F32),
        pltpu.VMEM((ch, wide), BF16),
        pltpu.VMEM((3,) + plane, F32),
        pltpu.VMEM((2, reach) + plane, BF16),
        pltpu.VMEM((2,) + plane, BF16),
        pltpu.VMEM((6,) + plane, BF16),
        pltpu.VMEM((2, npix, reach * lanes), BF16),
        pltpu.VMEM((2, npix, lanes), BF16),
        pltpu.VMEM((6, npix, lanes), BF16),
        pltpu.VMEM(plane, F32),
        pltpu.VMEM((n1, share, lanes), F32),
        pltpu.VMEM((share, lanes), F32),
        pltpu.VMEM((n2, share, lanes), F32),
        pltpu.VMEM((share, lanes), F32),
        pltpu.VMEM((n3, share, lanes), F32),
        pltpu.VMEM((share, lanes), F32),
        pltpu.VMEM((n1, share, lanes), F32),
        dma((nc,)),
        dma((nc,)),
        dma(()),
        dma((8,)),
        dma((8,)),
        dma((8,)),
        dma((8,)),
        dma((n1,)),
        dma((n1,)),
        dma((n2,)),
        dma((n2,)),
        dma((n3,)),
        dma((n3,)),
        dma((n1,)),
        dma((n1,)),
    ]
    stem, total = pl.pallas_call(
        functools.partial(body, place),
        out_shape=(
            jax.ShapeDtypeStruct((height,) + plane, BF16),
            jax.ShapeDtypeStruct(plane, F32),
        ),
        in_specs=[vmem] * 8,
        out_specs=(vmem, vmem),
        scratch_shapes=scratch,
        compiler_params=pltpu.CompilerParams(
            collective_id=0, has_side_effects=True, vmem_limit_bytes=40 << 20
        ),
    )(
        file_pixels.reshape(npix, wide),
        jnp.transpose(cotangent, (1, 0, 2)),
        patchify_weight,
        patchify_bias.reshape(1, ch),
        norm_gain.reshape(1, ch),
        norm_offset_vector.reshape(1, ch),
        kernel,
        kernel_offset.reshape(1, ch),
    )
    taps_at = 64
    after = taps_at + side * side
    return (
        jnp.transpose(stem, (1, 0, 2)),
        total[:, 0:npix],
        total[:, npix],
        total[:, after],
        total[:, after + 1],
        total[:, taps_at:after],
        total[:, after + 2],
    )


def solution(mesh, place=PLACE):
    return jax.shard_map(
        functools.partial(per_device, place),
        mesh=mesh,
        in_specs=(
            P(None, ("rows", "cols"), None),
            P(),
            P(),
            P(),
            P(),
            P(),
            P(),
            P(None, "rows", "cols"),
        ),
        out_specs=(P(None, "rows", "cols"), P(), P(), P(), P(), P(), P()),
        check_vma=False,
    )
```

time: 428 us -> 102 us (0.24); the launches traced: 420 us -> 102 us
  other arithmetic: 188 us -> 0 us
  blocking collectives: 124 us -> 0 us
  Pallas kernels: 0 us -> 95.2 us
  starting transfers between devices: 75.4 us -> 0 us
  local copies, waits for them, and re-layouts: 21.3 us -> 6.18 us
  waiting for transfers between devices: 7.75 us -> 0 us
    reduce_sum x8 -> x0, other arithmetic: 133 us -> none  [the longest x1 58.9 us: apply_layer_norm(): spread = jnp.mean(center * center, axis=0, keepdims=True)]
    psum x1 -> x0, blocking collectives: 124 us -> none  [per_device(): lax.psum((partial_weight, bias_part, norm_scale_gradient, shift_grad, ker...]
    pallas_call x0 -> x1, Pallas kernels: none -> 95.2 us  [per_device(): pl.pallas_call(functools.partial(body, place), out_shape=(jax.ShapeDtypeS...]
    ppermute x8 -> x0, starting transfers between devices: 41.2 us -> none  [the longest x4 23.7 us: extended(): lax.ppermute(lax.slice_in_dim(block, block.shape[dim] - width, None, axis...]
    all_to_all x2 -> x0, starting transfers between devices: 34.3 us -> none  [the longest x1 19.6 us: per_device(): lax.all_to_all(embed_patches(file_pixels, patchify_weight, patchify_bias)...]
    convert_element_type x3 -> x0, other arithmetic: 24.5 us -> none  [the longest x1 17.8 us: per_device(): stem_output = (depthwise(padded, kernel, height, breadth) + kernel_offset...]
    unnamed x1 -> x0, other arithmetic: 22.4 us -> none
    unnamed x157 -> x18, local copies, waits for them, and re-layouts: 14.2 us -> 5.36 us
  transfers between devices with their start and end apart: 10 -> 0, of which waited for: 3 -> 0; matrix products, arithmetic and copies ran while one was open for 13% -> 0% of each run, Pallas kernels for 0% -> 0%
where the time goes in v1:
time: 102 us
  Pallas kernels  95.2 us (93%)
  local copies, waits for them, and re-layouts  6.18 us (6%)
    pallas_call x1, Pallas kernels, per_device(): pl.pallas_call(functools.partial(body, place), out_shape=(jax.ShapeDtypeS...  95.2 us
    unnamed x18, local copies, waits for them, and re-layouts  5.36 us

profile of v1, /device:TPU:1, one launch (start us, length us, event | category | flops | bytes accessed | tf_op | source)
XLA Modules:
  0.0 102.1 jit_solution(4702582806581312964)
XLA Ops:
  0.6 0.0 copy-start.5
  0.6 0.8 copy.22.weight
  1.4 0.0 copy-done.5
  1.4 0.1 copy.23.kernel
  1.5 0.0 copy-start
  1.5 0.0 copy-start.4
  1.6 1.3 %copy.28 = bf16[64,32,128]{2,0,1:T(8,128)(2,1)S(1)} copy(bf16[64,32,128]{2,1,0:T(8,128)(2,1)} %param.15) | data formatting | bytes 1048576 | tf_op args[7]
  2.9 0.0 copy-start.1
  2.9 0.0 copy-start.2
  2.9 0.0 copy-start.3
  2.9 0.0 copy-done
  2.9 0.0 copy-done.4
  2.9 0.6 copy-done.1
  3.5 0.0 copy-done.2
  3.5 0.0 copy-done.3
  3.5 95.2 %shard_map.135 = (bf16[32,64,128]{2,1,0:T(8,128)(2,1)S(1)}, f32[64,128]{1,0:T(8,128)S(1)}) custom-call(bf16[48,4096]{1,0:T(8,128)(2,1)S(1)} %bitcast.13, bf16[32,64,128]{2,1,0:T(8,128)(2,1)S(1)} %bitcast.10, bf16[64,48]{1,0:T(8,128)(2,1)S(1)} %copy.22.weight, f32[1,64]{1,0:T(1,128)S(1)} %bitcast.14, f32[1,64]{1,0:T(1,128)S(1)} %bitcast.15, ...), custom_call_target="tpu_custom_call" | custom-call | tf_op jit(solution)/shard_map/pallas_call | solution.py:598
  98.8 1.1 %copy.24 = bf16[64,32,128]{2,1,0:T(8,128)(2,1)} copy(bf16[64,32,128]{2,0,1:T(8,128)(2,1)S(1)} %bitcast.12) | data formatting | bytes 1048576
  99.9 0.7 slice_reduce_fusion
  100.7 0.7 copy.25
  101.3 0.1 slice.22
  101.4 0.7 copy.26
Async XLA Ops:
  0.6 0.8 copy-start.5
  1.5 1.4 %copy-start = (bf16[48,1,4096]{2,0,1:T(8,128)(2,1)S(1)}, bf16[48,1,4096]{2,0,1:T(8,128)(2,1)}, u32[]{:S(2)}) copy-start(bf16[48,1,4096]{2,0,1:T(8,128)(2,1)} %param.8) | copy-start | bytes 1179652
  1.5 1.4 %copy-start.4 = (f32[64]{0:T(128)S(1)}, f32[64]{0:T(128)}, u32[]{:S(2)}) copy-start(f32[64]{0:T(128)} %param.14) | copy-start | bytes 772
  2.9 0.7 copy-start.1
  2.9 0.7 copy-start.2
  2.9 0.7 copy-start.3

commit v2 on v1

--- a/solution.py
+++ b/solution.py
@@ -22,34 +22,43 @@
 def body(
     place,
     pix,
-    cot,
-    weight,
-    bias,
-    gain,
-    shift,
-    kernel,
-    koff,
+    cot_in,
+    weight_in,
+    bias_in,
+    gain_in,
+    shift_in,
+    kernel_in,
+    koff_in,
     stem,
     total,
+    cot,
+    weight_t,
+    lines,
+    kernel,
+    weight,
+    cotf,
     pixb,
     up,
     uph,
     nor,
     norh,
-    xhat,
-    inv,
     ng,
     acc,
+    kgacc,
     taps,
     cols,
     pgb,
     sums,
+    uedge,
     urow,
+    upk,
     upack,
     upeer,
     prow,
     ppack,
     ppeer,
+    pnk,
+    turns,
     pay,
     rs,
     part,
@@ -58,6 +67,8 @@
     ey,
     part3,
     tot,
+    pay_out,
+    in_sem,
     a_send,
     a_recv,
     own_sem,
@@ -76,8 +87,7 @@
 ):
     nr = place["z_lo"] * place["x"]
     nc = place["y"] * place["z_hi"] * place["core"]
-    height = cot.shape[0]
-    ch = cot.shape[1]
+    ch, height = cot.shape[0], cot.shape[1]
     npix = pix.shape[0]
     tall = height + 2 * reach
     groups = ch // sub
@@ -111,16 +121,48 @@
     def peer3(m):
         return (row, y * (ncore * nzh) + m * ncore + core)
 
+    loads = [
+        pltpu.make_async_copy(source, target, in_sem.at[at])
+        for at, (source, target) in enumerate(
+            (
+                (cot_in, cot),
+                (kernel_in, kernel),
+                (weight_in, weight_t),
+                (bias_in, lines.at[0:1]),
+                (gain_in, lines.at[1:2]),
+                (shift_in, lines.at[2:3]),
+                (koff_in, lines.at[3:4]),
+            )
+        )
+    ]
+    for copy in loads:
+        copy.start()
+
     barrier = pltpu.get_barrier_semaphore()
 
     def greet(device):
         pl.semaphore_signal(barrier, inc=1, device_id=device, device_id_type=MESH)
 
-    def greet_col(d, carry):
-        greet((row, at_col(d)))
-        return carry
-
-    lax.fori_loop(1, nc, greet_col, 0)
+    far = sorted(range(nzh), key=lambda d: -min(d, nzh - d))
+    near_cols = ny * ncore
+
+    def col_of(dz, e):
+        return (
+            lax.rem(y + e // ncore, ny) * (ncore * nzh)
+            + lax.rem(zh + dz, nzh) * ncore
+            + lax.rem(core + lax.rem(e, ncore), ncore)
+        )
+
+    def each_col(act):
+        for dz in far:
+
+            def one(e, carry, dz=dz):
+                act(col_of(dz, e))
+                return carry
+
+            lax.fori_loop(1 if dz == 0 else 0, near_cols, one, 0)
+
+    each_col(lambda c: greet((row, c)))
     near = [(dr, dc) for dr in (-1, 1) for dc in (-1, 0, 1)]
     for dr, dc in near:
         greet((at_row(dr), at_col(dc)))
@@ -133,40 +175,53 @@
         greet(peer2(lax.rem(me2 + d, n2)))
         return carry
 
+    lax.fori_loop(1, n2, greet2, 0)
     lax.fori_loop(1, n1, greet1, 0)
-    lax.fori_loop(1, n2, greet2, 0)
 
     def pack(load, mask_lane, shape):
         def step(h, both):
             left, right = both
             v = load(h)
             at = 3 * h
-            left = jnp.where(
-                (mask_lane >= at) & (mask_lane < at + 3), pltpu.roll(v, at, 1), left
-            )
-            right = jnp.where(
-                (mask_lane >= 125 - at) & (mask_lane < 128 - at),
-                pltpu.roll(v, lanes - at, 1),
-                right,
-            )
+            here = (mask_lane >= at) & (mask_lane < at + 3)
+            left = jnp.where(here, pltpu.roll(v, at, 1), left)
+            right = jnp.where(here, pltpu.roll(v, at + 3, 1), right)
             return left, right
 
         zero = jnp.zeros(shape, F32)
-        v = load(0)
-        first = (
-            jnp.where(mask_lane < 3, v, zero),
-            jnp.where(mask_lane >= 125, v, zero),
-        )
-        return lax.fori_loop(1, height, step, first)
+        return lax.fori_loop(0, height, step, (zero, zero))
+
+    loads[0].wait()
+    for k in range(ch):
+        cotf[k * height : (k + 1) * height, :] = cot[k].astype(F32)
 
     def lift(h, carry):
-        up[h + reach] = cot[h].astype(F32)
+        up[h + reach] = cotf[pl.ds(h, ch, stride=height), :]
         return carry
 
     lax.fori_loop(0, height, lift, 0)
     left, right = pack(lambda h: up[h + reach], lane, (ch, lanes))
+    upk[0] = left
+    upk[1] = right
     upack[0] = left.astype(BF16)
     upack[1] = right.astype(BF16)
+    for k in range(reach):
+        uedge[k] = up[reach + k].astype(BF16)
+        uedge[reach + k] = up[height + k].astype(BF16)
+
+    for copy in loads[1:]:
+        copy.wait()
+    eye = lax.broadcasted_iota(jnp.int32, (ch, ch), 0) == lax.broadcasted_iota(
+        jnp.int32, (ch, ch), 1
+    )
+
+    def column(line):
+        spot = jnp.where(eye, jnp.broadcast_to(line, (ch, ch)), 0.0)
+        return jnp.broadcast_to(jnp.sum(spot, axis=1, keepdims=True), (ch, lanes))
+
+    for at in range(4):
+        cols[at] = column(lines[at : at + 1, :])
+    weight[...] = jnp.transpose(weight_t[...].astype(F32)).astype(BF16)
 
     pl.semaphore_wait(barrier, (nc - 1) + len(near) + (n1 - 1) + (n2 - 1))
 
@@ -205,7 +260,7 @@
         return copies
 
     u_copies = halo_copies(
-        cot.at[0:reach], cot.at[height - reach : height], upack, urow, upeer, u_send, u_recv
+        uedge.at[0:reach], uedge.at[reach : 2 * reach], upack, urow, upeer, u_send, u_recv
     )
     for copy in u_copies:
         copy.start()
@@ -213,45 +268,32 @@
     def block(c):
         return pl.ds(pl.multiple_of(c * lanes, lanes), lanes)
 
-    def send_pix(d):
-        target = at_col(d)
+    def send_pix(target):
         return pltpu.make_async_remote_copy(
             src_ref=pix.at[:, block(target)],
             dst_ref=pixb.at[0:npix, block(col)],
-            send_sem=a_send.at[d],
+            send_sem=a_send.at[target],
             recv_sem=a_recv.at[col],
             device_id=(row, target),
             device_id_type=MESH,
         )
 
-    def got_pix(d):
-        source = at_col(d)
+    def got_pix(source):
         return pltpu.make_async_remote_copy(
             src_ref=pix.at[:, block(col)],
             dst_ref=pixb.at[0:npix, block(source)],
-            send_sem=a_send.at[d],
+            send_sem=a_send.at[source],
             recv_sem=a_recv.at[source],
             device_id=(row, source),
             device_id_type=MESH,
         )
 
-    def start_pix(d, carry):
-        send_pix(d).start()
-        return carry
-
-    lax.fori_loop(1, nc, start_pix, 0)
+    each_col(lambda c: send_pix(c).start())
     own = pltpu.make_async_copy(pix.at[:, block(col)], pixb.at[0:npix, block(col)], own_sem)
     own.start()
 
-    eye = lax.broadcasted_iota(jnp.int32, (ch, ch), 0) == lax.broadcasted_iota(
-        jnp.int32, (ch, ch), 1
-    )
-    for at, ref in enumerate((bias, gain, shift, koff)):
-        line = jnp.broadcast_to(ref[...], (ch, ch))
-        column = jnp.sum(jnp.where(eye, line, 0.0), axis=1, keepdims=True)
-        cols[at] = jnp.broadcast_to(column, (ch, lanes))
     for tap in range(side * side):
-        taps[tap] = jnp.broadcast_to(kernel[:, tap : tap + 1], (ch, lanes))
+        taps[tap] = column(kernel[tap : tap + 1, :])
     extra = pixb.shape[0] - npix
     wide = pixb.shape[1]
     pixb[npix:, :] = jnp.where(
@@ -268,82 +310,69 @@
     top, bottom = row > 0, row < nr - 1
     west, east = col > 0, col < nc - 1
 
-    def spread(peer, out, width):
-        for at, (first, count, rows_ok) in enumerate(
-            ((height - reach, reach, top), (0, height, None), (0, reach, bottom))
-        ):
-            keep_l = west if rows_ok is None else west & rows_ok
-            keep_r = east if rows_ok is None else east & rows_ok
-            lo = jnp.where(keep_l, peer(at), 0.0)
-            hi = jnp.where(keep_r, peer(3 + at), 0.0)
-            base = (0, reach, reach + height)[at]
-
-            def one(k, carry, first=first, base=base, lo=lo, hi=hi):
-                h = first + k
-                out[base + k] = jnp.where(
-                    lane < 64,
-                    pltpu.roll(hi, lax.rem(lanes - 3 * h, lanes), 1),
-                    pltpu.roll(lo, 3 * h, 1),
-                )
-                return carry
-
-            lax.fori_loop(0, count, one, 0)
+    def join(peer, which):
+        keep = (west, east)[which]
+        end = 3 * height
+        own = pltpu.roll(peer(3 * which + 1), 9, 1)
+        above = pltpu.roll(peer(3 * which), lanes - (end - 9), 1)
+        below = pltpu.roll(peer(3 * which + 2), lax.rem(end + 9, lanes), 1)
+        first, middle = lane < 9, (lane >= 9) & (lane < end + 9)
+        final = (lane >= end + 9) & (lane < end + 18)
+        whole = jnp.where(middle & keep, own, 0.0)
+        whole = jnp.where(first & (keep & top), above, whole)
+        return jnp.where(final & (keep & bottom), below, whole)
+
+    def spread(packed, out):
+        lo, hi = packed[0], packed[1]
+        for a in range(tall):
+            out[a] = jnp.where(
+                lane < 64,
+                pltpu.roll(hi, (lanes - 3 * a) % lanes, 1),
+                pltpu.roll(lo, 125 - 3 * a, 1),
+            )
 
     for copy in u_copies:
         copy.wait_recv()
     for k in range(reach):
         up[k] = jnp.where(top, urow[0, k].astype(F32), 0.0)
         up[height + reach + k] = jnp.where(bottom, urow[1, k].astype(F32), 0.0)
-    spread(lambda slot: upeer[slot].astype(F32), uph, ch)
-
-    def sweep(src, halo, out, flip, kg):
+    for which in range(2):
+        pnk[which] = join(lambda slot: upeer[slot].astype(F32), which)
+    spread(pnk, uph)
+
+    def turned(j):
+        s = reach - j
+        return (lane8 >= lanes - s) | (lane8 < -s), lax.rem(s + lanes, lanes)
+
+    def sweep(src, halo, out, flip, first, final):
         def one(step, carry):
             g, j = step // side, lax.rem(step, side)
             gs = pl.ds(pl.multiple_of(g * sub, sub), sub)
-            s = reach - j
-            mask = (lane8 >= lanes - s) | (lane8 < -s)
-            amount = lax.rem(s + lanes, lanes)
+            mask, amount = turned(j)
             if flip:
                 t = [taps[(side - 1 - i) * side + (side - 1 - j), gs] for i in range(side)]
             else:
                 t = [taps[i * side + j, gs] for i in range(side)]
-            sumk = [None] * side
             live = {}
-            us = {}
             for a in range(tall):
                 v = pltpu.roll(jnp.where(mask, halo[a, gs], src[a, gs]), amount, 1)
                 if a < height:
                     live[a] = out[a, gs]
-                    if kg:
-                        us[a] = up[a + reach, gs]
                 for i in range(side):
                     h = a - i
                     if 0 <= h < height:
                         live[h] = live[h] + t[i] * v
-                        if kg:
-                            term = us[h] * v
-                            sumk[i] = term if sumk[i] is None else sumk[i] + term
                 h = a - (side - 1)
                 if h >= 0:
                     out[h, gs] = live.pop(h)
-                    us.pop(h, None)
-            if kg:
-                line = pay[gs]
-                for i in range(side):
-                    line = jnp.where(
-                        lane8 == 64 + i * side + j,
-                        jnp.sum(sumk[i], axis=1, keepdims=True) * factor,
-                        line,
-                    )
-                pay[gs] = line
             return carry
 
-        lax.fori_loop(0, groups * side, one, 0)
-
-    sweep(up, uph, ng, True, False)
+        lax.fori_loop(first * side, final * side, one, 0)
+
+    sweep(up, uph, ng, True, 0, groups)
 
     def wait_pix(d, carry):
-        got_pix(d).wait_recv()
+        got_pix(at_col(d)).wait_recv()
         return carry
 
     lax.fori_loop(1, nc, wait_pix, 0)
@@ -375,25 +404,50 @@
 
     sums[...] = jnp.zeros_like(sums)
 
-    def inner(h, carry):
-        hat, deviation = embed(pixb[0:npix, block(h)])
-        nor[h + reach] = finish(hat)
-        grad = ng[h] * factor
-        sums[0] += grad * hat
-        sums[1] += grad
-        sums[2] += up[h + reach]
-        xgrad = grad * cols[1]
-        mean1 = jnp.mean(xgrad, axis=0, keepdims=True)
-        mean2 = jnp.mean(xgrad * hat, axis=0, keepdims=True)
-        pgb[:, block(h)] = (deviation * (xgrad - mean1 - hat * mean2)).astype(BF16)
-        return carry
-
-    lax.fori_loop(0, height, inner, 0)
+    def inner(pair, carry):
+        for k in range(2):
+            h = 2 * pair + k
+            hat, deviation = embed(pixb[0:npix, block(h)])
+            nor[h + reach] = finish(hat)
+            grad = ng[h] * factor
+            sums[0, k] += grad * hat
+            sums[1, k] += grad
+            sums[2, k] += up[h + reach]
+            xgrad = grad * cols[1]
+            mean1 = jnp.mean(xgrad, axis=0, keepdims=True)
+            mean2 = jnp.mean(xgrad * hat, axis=0, keepdims=True)
+            pgb[:, block(h)] = (deviation * (xgrad - mean1 - hat * mean2)).astype(BF16)
+        return carry
+
+    lax.fori_loop(0, height // 2, inner, 0)
     grads = lax.dot_general(
         pgb[...], pixb[...], (((1,), (1,)), ((), ())), preferred_element_type=F32
     )
     pay[...] = jnp.zeros_like(pay)
     pay[:, 0 : pixb.shape[0]] = grads
+
+    def kg_inner(step, carry):
+        g, j = step // side, lax.rem(step, side)
+        gs = pl.ds(pl.multiple_of(g * sub, sub), sub)
+        mask, amount = turned(j)
+        sumk = [None] * side
+        us = {}
+        for a in range(tall - reach):
+            if a < height:
+                us[a] = up[a + reach, gs]
+            if a >= reach:
+                v = pltpu.roll(jnp.where(mask, 0.0, nor[a, gs]), amount, 1)
+                for i in range(side):
+                    h = a - i
+                    if 0 <= h < height:
+                        term = us[h] * v
+                        sumk[i] = term if sumk[i] is None else sumk[i] + term
+            us.pop(a - (side - 1), None)
+        for i in range(side):
+            kgacc[i * side + j, gs] = sumk[i]
+        return carry
+
+    lax.fori_loop(0, groups * side, kg_inner, 0)
 
     for copy in p_copies:
         copy.wait_recv()
@@ -401,23 +455,78 @@
         ks = slice(k * lanes, (k + 1) * lanes)
         nor[k] = jnp.where(top, finish(embed(prow[0, :, ks])[0]), 0.0)
         nor[height + reach + k] = jnp.where(bottom, finish(embed(prow[1, :, ks])[0]), 0.0)
-    spread(lambda slot: finish(embed(ppeer[slot])[0]), norh, ch)
-
-    sweep(nor, norh, acc, False, True)
+    for which in range(2):
+        pnk[which] = join(lambda slot: finish(embed(ppeer[slot])[0]), which)
+    for at in range(3 * side):
+        turns[0, at] = pltpu.roll(pnk[0], (-at) % lanes, 1)
+        turns[1, at] = pltpu.roll(pnk[1], (2 - at) % lanes, 1)
+    outer = [(a, i) for a in range(tall) for i in range(side) if 0 <= a - i < height]
+    outer = [(a, i) for a, i in outer if a < reach or a >= height + reach]
+    lane16 = lax.broadcasted_iota(jnp.int32, (2 * sub, lanes), 1)
+    place3 = lax.rem(lane16, 3)
+
+    def kg_outer(g, carry):
+        gs = pl.ds(pl.multiple_of(g * 2 * sub, 2 * sub), 2 * sub)
+        for j in range(side):
+            s = reach - j
+            v = {}
+            for a in sorted({a for a, _ in outer}):
+                v[a] = nor[a, gs]
+                if s > 0:
+                    v[a] = jnp.where(lane16 >= lanes - s, 0.0, v[a])
+                if s < 0:
+                    v[a] = jnp.where(lane16 < -s, 0.0, v[a])
+                v[a] = pltpu.roll(v[a], s % lanes, 1)
+            if s > 0:
+                edge = jnp.where(place3 < s, upk[0, gs], 0.0)
+            if s < 0:
+                edge = jnp.where(place3 >= reach + s, upk[1, gs], 0.0)
+            for i in range(side):
+                whole = kgacc[i * side + j, gs]
+                for a, tap_row in outer:
+                    if tap_row == i:
+                        whole = whole + up[a - i + reach, gs] * v[a]
+                if s > 0:
+                    whole = whole + edge * turns[0, 3 * i + j, gs]
+                if s < 0:
+                    whole = whole + edge * turns[1, 3 * i + j - 4, gs]
+                kgacc[i * side + j, gs] = whole
+        return carry
+
+    lax.fori_loop(0, ch // (2 * sub), kg_outer, 0)
+    ones = jnp.ones((lanes, lanes), BF16)
+    for at, scale in ((0, 1.0 / factor), (1, 1.0 / factor), (2, 1.0)):
+        kgacc[side * side + at] = (sums[at, 0] + sums[at, 1]) * scale
+    whole = pay[...]
+    for first in range(0, side * side + 3, side):
+        count = min(side, side * side + 3 - first)
+        value = kgacc[first : first + count].reshape(count * ch, lanes)
+        high = value.astype(BF16)
+        low = (value - high.astype(F32)).astype(BF16)
+        lines_of = jnp.dot(high, ones, preferred_element_type=F32)
+        lines_of += jnp.dot(low, ones, preferred_element_type=F32)
+        for k in range(count):
+            whole = jnp.where(
+                lane == 64 + first + k, lines_of[k * ch : (k + 1) * ch] * factor, whole
+            )
+    pay[...] = whole
 
     def close(h, carry):
         stem[h] = acc[h].astype(BF16)
         return carry
 
-    lax.fori_loop(0, height, close, 0)
-    last = pay[...]
-    for at, scale in ((0, 1.0), (1, 1.0), (2, factor)):
-        last = jnp.where(
-            lane == 64 + side * side + at,
-            jnp.sum(sums[at], axis=1, keepdims=True) * scale,
-            last,
-        )
-    pay[...] = last
+    def piece1():
+        spread(pnk, norh)
+        sweep(nor, norh, acc, False, 0, 1)
+
+    def piece2():
+        sweep(nor, norh, acc, False, 1, 4)
+
+    def piece3():
+        sweep(nor, norh, acc, False, 4, groups)
+
+    def piece4():
+        lax.fori_loop(0, height, close, 0)
 
     share = ch // n1
 
@@ -446,7 +555,7 @@
             device_id_type=MESH,
         )
 
-    def exchange(source, slots, me, n, peer, send, recv):
+    def exchange(source, slots, me, n, peer, send, recv, meanwhile):
         def put(d):
             m = lax.rem(me + d, n)
             return pltpu.make_async_remote_copy(
@@ -483,6 +592,7 @@
 
         lax.fori_loop(1, n, start, 0)
         slots[me] = source[...]
+        meanwhile()
         lax.fori_loop(1, n, arrive, 0)
         return lambda: lax.fori_loop(1, n, sent, 0)
 
@@ -500,6 +610,7 @@
 
     lax.fori_loop(1, n1, start1, 0)
     rs[me1] = pay[rows_of(me1)]
+    piece1()
     lax.fori_loop(1, n1, arrive1, 0)
 
     def sum_of(slots, n):
@@ -509,16 +620,17 @@
         return whole
 
     part[...] = sum_of(rs, n1)
-    done2 = exchange(part, ex, me2, n2, peer2, e_send, e_recv)
+    done2 = exchange(part, ex, me2, n2, peer2, e_send, e_recv, piece2)
     part2[...] = sum_of(ex, n2)
-    done3 = exchange(part2, ey, me3, n3, peer3, z_send, z_recv)
+    done3 = exchange(part2, ey, me3, n3, peer3, z_send, z_recv, piece3)
     part3[...] = sum_of(ey, n3)
-    done4 = exchange(part3, tot, me1, n1, peer1, g_send, g_recv)
+    done4 = exchange(part3, tot, me1, n1, peer1, g_send, g_recv, piece4)
     for k in range(n1):
-        total[k * share : (k + 1) * share, :] = tot[k]
+        pay_out[k * share : (k + 1) * share, :] = tot[k]
+    total[...] = jnp.transpose(pay_out[...])
 
     def sent_pix(d, carry):
-        send_pix(d).wait_send()
+        send_pix(at_col(d)).wait_send()
         return carry
 
     lax.fori_loop(1, nc, sent_pix, 0)
@@ -552,25 +664,34 @@
     vmem = pl.BlockSpec(memory_space=pltpu.VMEM)
     dma = pltpu.SemaphoreType.DMA
     scratch = [
+        pltpu.VMEM((ch, height, lanes), BF16),
+        pltpu.VMEM((npix, ch), BF16),
+        pltpu.VMEM((sub, ch), F32),
+        pltpu.VMEM((side * side, ch), F32),
+        pltpu.VMEM((ch, npix), BF16),
+        pltpu.VMEM((ch * height, lanes), F32),
         pltpu.VMEM((64, wide), BF16),
         pltpu.VMEM((tall,) + plane, F32),
         pltpu.VMEM((tall,) + plane, F32),
         pltpu.VMEM((tall,) + plane, F32),
         pltpu.VMEM((tall,) + plane, F32),
-        pltpu.VMEM((1,) + plane, F32),
-        pltpu.VMEM((sub, lanes), F32),
         pltpu.VMEM((height,) + plane, F32),
         pltpu.VMEM((height,) + plane, F32),
+        pltpu.VMEM((side * side + 3,) + plane, F32),
         pltpu.VMEM((side * side,) + plane, F32),
         pltpu.VMEM((4,) + plane, F32),
         pltpu.VMEM((ch, wide), BF16),
-        pltpu.VMEM((3,) + plane, F32),
+        pltpu.VMEM((3, 2) + plane, F32),
+        pltpu.VMEM((2 * reach,) + plane, BF16),
         pltpu.VMEM((2, reach) + plane, BF16),
+        pltpu.VMEM((2,) + plane, F32),
         pltpu.VMEM((2,) + plane, BF16),
         pltpu.VMEM((6,) + plane, BF16),
         pltpu.VMEM((2, npix, reach * lanes), BF16),
         pltpu.VMEM((2, npix, lanes), BF16),
         pltpu.VMEM((6, npix, lanes), BF16),
+        pltpu.VMEM((2,) + plane, F32),
+        pltpu.VMEM((2, 3 * side) + plane, F32),
         pltpu.VMEM(plane, F32),
         pltpu.VMEM((n1, share, lanes), F32),
         pltpu.VMEM((share, lanes), F32),
@@ -579,6 +700,8 @@
         pltpu.VMEM((n3, share, lanes), F32),
         pltpu.VMEM((share, lanes), F32),
         pltpu.VMEM((n1, share, lanes), F32),
+        pltpu.VMEM(plane, F32),
+        dma((7,)),
         dma((nc,)),
         dma((nc,)),
         dma(()),
@@ -599,9 +722,9 @@
         functools.partial(body, place),
         out_shape=(
             jax.ShapeDtypeStruct((height,) + plane, BF16),
-            jax.ShapeDtypeStruct(plane, F32),
+            jax.ShapeDtypeStruct((lanes, ch), F32),
         ),
-        in_specs=[vmem] * 8,
+        in_specs=[pl.BlockSpec(memory_space=pltpu.HBM)] * 8,
         out_specs=(vmem, vmem),
         scratch_shapes=scratch,
         compiler_params=pltpu.CompilerParams(
@@ -609,24 +732,24 @@
         ),
     )(
         file_pixels.reshape(npix, wide),
-        jnp.transpose(cotangent, (1, 0, 2)),
-        patchify_weight,
+        cotangent,
+        patchify_weight.T,
         patchify_bias.reshape(1, ch),
         norm_gain.reshape(1, ch),
         norm_offset_vector.reshape(1, ch),
-        kernel,
+        kernel.T,
         kernel_offset.reshape(1, ch),
     )
     taps_at = 64
     after = taps_at + side * side
     return (
         jnp.transpose(stem, (1, 0, 2)),
-        total[:, 0:npix],
-        total[:, npix],
-        total[:, after],
-        total[:, after + 1],
-        total[:, taps_at:after],
-        total[:, after + 2],
+        total[0:npix].T,
+        total[npix],
+        total[after],
+        total[after + 1],
+        total[taps_at:after].T,
+        total[after + 2],
     )
 
 

time: 102 us -> 89.9 us (0.88)
  Pallas kernels: 95.2 us -> 81.2 us
  local copies, waits for them, and re-layouts: 6.18 us -> 7.66 us
    pallas_call x1, Pallas kernels: 95.2 us -> 81.2 us  [per_device(): pl.pallas_call(functools.partial(body, place), out_shape=(jax.ShapeDtypeS...]
    transpose x0 -> x2, local copies, waits for them, and re-layouts: none -> 1.22 us  [the longest x1 0.61 us: per_device(): total[taps_at:after]]
    unnamed x18 -> x17, local copies, waits for them, and re-layouts: 5.36 us -> 5.92 us
where the time goes in v2:
time: 89.9 us; the launch traced here: 89.5 us
  Pallas kernels  81.2 us (90%)
  local copies, waits for them, and re-layouts  7.66 us (9%)
    pallas_call x1, Pallas kernels, per_device(): pl.pallas_call(functools.partial(body, place), out_shape=(jax.ShapeDtypeS...  81.2 us
    unnamed x17, local copies, waits for them, and re-layouts  5.92 us

profile of v2, /device:TPU:1, one launch (start us, length us, event | category | flops | bytes accessed | tf_op | source)
XLA Modules:
  0.0 89.5 jit_solution(10715468040519469675)
XLA Ops:
  0.6 0.0 copy-start.3
  0.6 0.0 copy-start.4
  0.7 0.0 copy-start.5
  0.7 0.7 copy-done.3
  1.3 0.0 copy-done.4
  1.3 0.0 copy-done.5
  1.3 0.0 copy-start
  1.4 1.0 %copy-done = bf16[64,32,128]{2,1,0:T(8,128)(2,1)S(1)} copy-done((bf16[64,32,128]{2,1,0:T(8,128)(2,1)S(1)}, bf16[64,32,128]{2,1,0:T(8,128)(2,1)}, u32[]{:S(2)}) %copy-start) | copy-done | bytes 524312
  2.4 0.0 copy-start.1
  2.4 1.0 %copy-done.1 = bf16[48,1,4096]{2,0,1:T(8,128)(2,1)S(1)} copy-done((bf16[48,1,4096]{2,0,1:T(8,128)(2,1)S(1)}, bf16[48,1,4096]{2,0,1:T(8,128)(2,1)}, u32[]{:S(2)}) %copy-start.1) | copy-done | bytes 393240
  3.4 0.0 copy-start.2
  3.4 0.7 copy-done.2
  4.1 0.0 copy-start.6
  4.1 0.7 copy-done.6
  4.8 0.0 copy-start.7
  4.8 0.7 copy-done.7
  5.4 81.2 %shard_map.135 = (bf16[32,64,128]{2,1,0:T(8,128)(2,1)S(1)}, f32[128,64]{1,0:T(8,128)S(1)}) custom-call(bf16[48,4096]{1,0:T(8,128)(2,1)S(1)} %bitcast.21, bf16[64,32,128]{2,1,0:T(8,128)(2,1)S(1)} %copy-done, bf16[48,64]{1,0:T(8,128)(2,1)S(1)} %bitcast.23, f32[1,64]{1,0:T(1,128)S(1)} %bitcast.24, f32[1,64]{1,0:T(1,128)S(1)} %bitcast.25, f32[1,64]{1,0:T(1,128)S(1)} %bitcast.26, ...), custom_call_target="tpu_custom_call" | custom-call | tf_op jit(solution)/shard_map/pallas_call | solution.py:721
  86.6 0.5 slice_bitcast_fusion.2
  87.2 0.6 slice_bitcast_fusion
  87.8 0.6 slice_bitcast_fusion.1
  88.4 1.1 %copy.15 = bf16[64,32,128]{2,1,0:T(8,128)(2,1)} copy(bf16[64,32,128]{2,0,1:T(8,128)(2,1)S(1)} %bitcast.20) | data formatting | bytes 1048576
Async XLA Ops:
  0.6 0.7 copy-start.3
  0.6 0.7 copy-start.4
  0.7 0.7 copy-start.5
  1.3 1.0 %copy-start = (bf16[64,32,128]{2,1,0:T(8,128)(2,1)S(1)}, bf16[64,32,128]{2,1,0:T(8,128)(2,1)}, u32[]{:S(2)}) copy-start(bf16[64,32,128]{2,1,0:T(8,128)(2,1)} %cot_in.1) | copy-start | bytes 1572868
  2.4 1.0 %copy-start.1 = (bf16[48,1,4096]{2,0,1:T(8,128)(2,1)S(1)}, bf16[48,1,4096]{2,0,1:T(8,128)(2,1)}, u32[]{:S(2)}) copy-start(bf16[48,1,4096]{2,0,1:T(8,128)(2,1)} %param.8) | copy-start | bytes 1179652
  3.4 0.7 copy-start.2
  4.1 0.7 copy-start.6
  4.8 0.7 copy-start.7

commit v3 on v2

--- a/solution.py
+++ b/solution.py
@@ -39,7 +39,6 @@
     cotf,
     pixb,
     up,
-    uph,
     nor,
     norh,
     ng,
@@ -331,20 +330,18 @@
                 pltpu.roll(lo, 125 - 3 * a, 1),
             )
 
-    for copy in u_copies:
-        copy.wait_recv()
-    for k in range(reach):
-        up[k] = jnp.where(top, urow[0, k].astype(F32), 0.0)
-        up[height + reach + k] = jnp.where(bottom, urow[1, k].astype(F32), 0.0)
-    for which in range(2):
-        pnk[which] = join(lambda slot: upeer[slot].astype(F32), which)
-    spread(pnk, uph)
-
     def turned(j):
         s = reach - j
         return (lane8 >= lanes - s) | (lane8 < -s), lax.rem(s + lanes, lanes)
 
+    outer = [(a, i) for a in range(tall) for i in range(side) if 0 <= a - i < height]
+    outer = [(a, i) for a, i in outer if a < reach or a >= height + reach]
+    lane16 = lax.broadcasted_iota(jnp.int32, (2 * sub, lanes), 1)
+    place3 = lax.rem(lane16, 3)
+
     def sweep(src, halo, out, flip, first, final):
+        inside = range(tall) if halo is not None else range(reach, height + reach)
+
         def one(step, carry):
             g, j = step // side, lax.rem(step, side)
             gs = pl.ds(pl.multiple_of(g * sub, sub), sub)
@@ -355,13 +352,15 @@
                 t = [taps[i * side + j, gs] for i in range(side)]
             live = {}
             for a in range(tall):
-                v = pltpu.roll(jnp.where(mask, halo[a, gs], src[a, gs]), amount, 1)
                 if a < height:
                     live[a] = out[a, gs]
-                for i in range(side):
-                    h = a - i
-                    if 0 <= h < height:
-                        live[h] = live[h] + t[i] * v
+                if a in inside:
+                    beyond = 0.0 if halo is None else halo[a, gs]
+                    v = pltpu.roll(jnp.where(mask, beyond, src[a, gs]), amount, 1)
+                    for i in range(side):
+                        h = a - i
+                        if 0 <= h < height:
+                            live[h] = live[h] + t[i] * v
                 h = a - (side - 1)
                 if h >= 0:
                     out[h, gs] = live.pop(h)
@@ -369,17 +368,115 @@
 
         lax.fori_loop(first * side, final * side, one, 0)
 
-    sweep(up, uph, ng, True, 0, groups)
-
-    def wait_pix(d, carry):
-        got_pix(at_col(d)).wait_recv()
-        return carry
-
-    lax.fori_loop(1, nc, wait_pix, 0)
+    def shifted_rows(src, gs, j):
+        s = reach - j
+        v = {}
+        for a in sorted({a for a, _ in outer}):
+            v[a] = src[a, gs]
+            if s > 0:
+                v[a] = jnp.where(lane16 >= lanes - s, 0.0, v[a])
+            if s < 0:
+                v[a] = jnp.where(lane16 < -s, 0.0, v[a])
+            v[a] = pltpu.roll(v[a], s % lanes, 1)
+        return v
+
+    def turn(load):
+        for which in range(2):
+            pnk[which] = join(load, which)
+        for at in range(3 * side):
+            turns[0, at] = pltpu.roll(pnk[0], (-at) % lanes, 1)
+            turns[1, at] = pltpu.roll(pnk[1], (2 - at) % lanes, 1)
+
+    sweep(up, None, ng, True, 0, groups)
+    for copy in u_copies:
+        copy.wait_recv()
+    for k in range(reach):
+        up[k] = jnp.where(top, urow[0, k].astype(F32), 0.0)
+        up[height + reach + k] = jnp.where(bottom, urow[1, k].astype(F32), 0.0)
+    turn(lambda slot: upeer[slot].astype(F32))
+    rims = sorted({a - i for a, i in outer})
+
+    def ng_outer(g, carry):
+        gs = pl.ds(pl.multiple_of(g * 2 * sub, 2 * sub), 2 * sub)
+        live = {h: ng[h, gs] for h in rims}
+        lo = jnp.zeros((2 * sub, lanes), F32)
+        hi = jnp.zeros((2 * sub, lanes), F32)
+        for j in range(side):
+            v = shifted_rows(up, gs, j)
+            for i in range(side):
+                t = taps[(side - 1 - i) * side + (side - 1 - j), gs]
+                for a, tap_row in outer:
+                    if tap_row == i:
+                        live[a - i] = live[a - i] + t * v[a]
+                if j < reach:
+                    lo = lo + jnp.where(place3 < reach - j, t * turns[0, 3 * i + j, gs], 0.0)
+                if j > reach:
+                    hi = hi + jnp.where(
+                        place3 >= 2 * reach - j, t * turns[1, 3 * i + j - 4, gs], 0.0
+                    )
+        for h in rims:
+            ng[h, gs] = live[h]
+        pnk[0, gs] = lo
+        pnk[1, gs] = hi
+        return carry
+
+    lax.fori_loop(0, ch // (2 * sub), ng_outer, 0)
+    lo, hi = pnk[0], pnk[1]
+    for h in range(height):
+        ng[h] += jnp.where(
+            lane < reach,
+            pltpu.roll(lo, (-3 * h) % lanes, 1),
+            jnp.where(lane >= lanes - reach, pltpu.roll(hi, (125 - 3 * h) % lanes, 1), 0.0),
+        )
+
     own.wait()
-    left, right = pack(lambda h: pixb[0:npix, block(h)].astype(F32), lanep, (npix, lanes))
-    ppack[0] = left.astype(BF16)
-    ppack[1] = right.astype(BF16)
+
+    def embed(pixels):
+        patch = jnp.dot(weight[...], pixels, preferred_element_type=F32) + cols[0]
+        v = patch.astype(BF16).astype(F32)
+        center = v - jnp.mean(v, axis=0, keepdims=True)
+        deviation = lax.rsqrt(jnp.mean(center * center, axis=0, keepdims=True) + norm_eps)
+        return center * deviation, deviation
+
+    def finish(hat):
+        return (hat * cols[1] + cols[2]).astype(BF16).astype(F32)
+
+    sums[...] = jnp.zeros_like(sums)
+
+    def inner(dz, e, both):
+        c0 = col_of(dz, ncore * e) - core
+        left, right = both
+        for k in range(ncore):
+            h = c0 + k
+
+            @pl.when(h != col)
+            def _(h=h):
+                got_pix(h).wait_recv()
+
+        for k in range(ncore):
+            h = c0 + k
+            pixels = pixb[0:npix, block(h)]
+            v = pixels.astype(F32)
+            here = (lanep >= 3 * h) & (lanep < 3 * h + 3)
+            left = jnp.where(here, pltpu.roll(v, 3 * h, 1), left)
+            right = jnp.where(here, pltpu.roll(v, 3 * h + 3, 1), right)
+            hat, deviation = embed(pixels)
+            nor[h + reach] = finish(hat)
+            grad = ng[h] * factor
+            sums[0, k] += grad * hat
+            sums[1, k] += grad
+            sums[2, k] += up[h + reach]
+            xgrad = grad * cols[1]
+            mean1 = jnp.mean(xgrad, axis=0, keepdims=True)
+            mean2 = jnp.mean(xgrad * hat, axis=0, keepdims=True)
+            pgb[:, block(h)] = (deviation * (xgrad - mean1 - hat * mean2)).astype(BF16)
+        return left, right
+
+    edges = (jnp.zeros((npix, lanes), F32), jnp.zeros((npix, lanes), F32))
+    for dz in far[::-1]:
+        edges = lax.fori_loop(0, ny, functools.partial(lambda dz, e, b: inner(dz, e, b), dz), edges)
+    ppack[0] = edges[0].astype(BF16)
+    ppack[1] = edges[1].astype(BF16)
     p_copies = halo_copies(
         pixb.at[0:npix, 0 : reach * lanes],
         pixb.at[0:npix, (height - reach) * lanes : height * lanes],
@@ -392,34 +489,6 @@
     for copy in p_copies:
         copy.start()
 
-    def embed(pixels):
-        patch = jnp.dot(weight[...], pixels, preferred_element_type=F32) + cols[0]
-        v = patch.astype(BF16).astype(F32)
-        center = v - jnp.mean(v, axis=0, keepdims=True)
-        deviation = lax.rsqrt(jnp.mean(center * center, axis=0, keepdims=True) + norm_eps)
-        return center * deviation, deviation
-
-    def finish(hat):
-        return (hat * cols[1] + cols[2]).astype(BF16).astype(F32)
-
-    sums[...] = jnp.zeros_like(sums)
-
-    def inner(pair, carry):
-        for k in range(2):
-            h = 2 * pair + k
-            hat, deviation = embed(pixb[0:npix, block(h)])
-            nor[h + reach] = finish(hat)
-            grad = ng[h] * factor
-            sums[0, k] += grad * hat
-            sums[1, k] += grad
-            sums[2, k] += up[h + reach]
-            xgrad = grad * cols[1]
-            mean1 = jnp.mean(xgrad, axis=0, keepdims=True)
-            mean2 = jnp.mean(xgrad * hat, axis=0, keepdims=True)
-            pgb[:, block(h)] = (deviation * (xgrad - mean1 - hat * mean2)).astype(BF16)
-        return carry
-
-    lax.fori_loop(0, height // 2, inner, 0)
     grads = lax.dot_general(
         pgb[...], pixb[...], (((1,), (1,)), ((), ())), preferred_element_type=F32
     )
@@ -455,28 +524,13 @@
         ks = slice(k * lanes, (k + 1) * lanes)
         nor[k] = jnp.where(top, finish(embed(prow[0, :, ks])[0]), 0.0)
         nor[height + reach + k] = jnp.where(bottom, finish(embed(prow[1, :, ks])[0]), 0.0)
-    for which in range(2):
-        pnk[which] = join(lambda slot: finish(embed(ppeer[slot])[0]), which)
-    for at in range(3 * side):
-        turns[0, at] = pltpu.roll(pnk[0], (-at) % lanes, 1)
-        turns[1, at] = pltpu.roll(pnk[1], (2 - at) % lanes, 1)
-    outer = [(a, i) for a in range(tall) for i in range(side) if 0 <= a - i < height]
-    outer = [(a, i) for a, i in outer if a < reach or a >= height + reach]
-    lane16 = lax.broadcasted_iota(jnp.int32, (2 * sub, lanes), 1)
-    place3 = lax.rem(lane16, 3)
+    turn(lambda slot: finish(embed(ppeer[slot])[0]))
 
     def kg_outer(g, carry):
         gs = pl.ds(pl.multiple_of(g * 2 * sub, 2 * sub), 2 * sub)
         for j in range(side):
             s = reach - j
-            v = {}
-            for a in sorted({a for a, _ in outer}):
-                v[a] = nor[a, gs]
-                if s > 0:
-                    v[a] = jnp.where(lane16 >= lanes - s, 0.0, v[a])
-                if s < 0:
-                    v[a] = jnp.where(lane16 < -s, 0.0, v[a])
-                v[a] = pltpu.roll(v[a], s % lanes, 1)
+            v = shifted_rows(nor, gs, j)
             if s > 0:
                 edge = jnp.where(place3 < s, upk[0, gs], 0.0)
             if s < 0:
@@ -512,7 +566,7 @@
     pay[...] = whole
 
     def close(h, carry):
-        stem[h] = acc[h].astype(BF16)
+        cotf[pl.ds(h, ch, stride=height), :] = acc[h]
         return carry
 
     def piece1():
@@ -527,6 +581,8 @@
 
     def piece4():
         lax.fori_loop(0, height, close, 0)
+        for k in range(ch):
+            stem[k] = cotf[k * height : (k + 1) * height, :].astype(BF16)
 
     share = ch // n1
 
@@ -671,7 +727,6 @@
         pltpu.VMEM((ch, npix), BF16),
         pltpu.VMEM((ch * height, lanes), F32),
         pltpu.VMEM((64, wide), BF16),
-        pltpu.VMEM((tall,) + plane, F32),
         pltpu.VMEM((tall,) + plane, F32),
         pltpu.VMEM((tall,) + plane, F32),
         pltpu.VMEM((tall,) + plane, F32),
@@ -721,7 +776,7 @@
     stem, total = pl.pallas_call(
         functools.partial(body, place),
         out_shape=(
-            jax.ShapeDtypeStruct((height,) + plane, BF16),
+            jax.ShapeDtypeStruct((ch, height, lanes), BF16),
             jax.ShapeDtypeStruct((lanes, ch), F32),
         ),
         in_specs=[pl.BlockSpec(memory_space=pltpu.HBM)] * 8,
@@ -731,19 +786,24 @@
             collective_id=0, has_side_effects=True, vmem_limit_bytes=40 << 20
         ),
     )(
-        file_pixels.reshape(npix, wide),
-        cotangent,
-        patchify_weight.T,
-        patchify_bias.reshape(1, ch),
-        norm_gain.reshape(1, ch),
-        norm_offset_vector.reshape(1, ch),
-        kernel.T,
-        kernel_offset.reshape(1, ch),
+        *(
+            pltpu.with_memory_space_constraint(value, pltpu.HBM)
+            for value in (
+                file_pixels.reshape(npix, wide),
+                cotangent,
+                patchify_weight.T,
+                patchify_bias.reshape(1, ch),
+                norm_gain.reshape(1, ch),
+                norm_offset_vector.reshape(1, ch),
+                kernel.T,
+                kernel_offset.reshape(1, ch),
+            )
+        )
     )
     taps_at = 64
     after = taps_at + side * side
     return (
-        jnp.transpose(stem, (1, 0, 2)),
+        stem,
         total[0:npix].T,
         total[npix],
         total[after],

time: 89.9 us -> 79.7 us (0.89)
  local copies, waits for them, and re-layouts: 7.66 us -> 2.54 us
  Pallas kernels: 81.2 us -> 76.4 us
    unnamed x17 -> x1, local copies, waits for them, and re-layouts: 5.92 us -> 0.79 us
    pallas_call x1, Pallas kernels: 81.2 us -> 76.4 us  [per_device(): pl.pallas_call(functools.partial(body, place), out_shape=(jax.ShapeDtypeS...]
where the time goes in v3:
time: 79.7 us; the launch traced here: 79.6 us
  Pallas kernels  76.4 us (96%)
  local copies, waits for them, and re-layouts  2.54 us (3%)
    pallas_call x1, Pallas kernels, per_device(): pl.pallas_call(functools.partial(body, place), out_shape=(jax.ShapeDtypeS...  76.4 us

profile of v3, /device:TPU:1, one launch (start us, length us, event | category | flops | bytes accessed | tf_op | source)
XLA Modules:
  0.0 79.6 jit_solution(2950507170563314393)
XLA Ops:
  0.6 76.4 %shard_map.135 = (bf16[64,32,128]{2,1,0:T(8,128)(2,1)S(1)}, f32[128,64]{1,0:T(8,128)S(1)}) custom-call(bf16[48,4096]{1,0:T(8,128)(2,1)} %bitcast.19, bf16[64,32,128]{2,1,0:T(8,128)(2,1)} %cot_in.1, bf16[48,64]{1,0:T(8,128)(2,1)} %bitcast.21, f32[1,64]{1,0:T(1,128)} %bitcast.22, f32[1,64]{1,0:T(1,128)} %bitcast.23, f32[1,64]{1,0:T(1,128)} %bitcast.24, ...), custom_call_target="tpu_custom_call" | custom-call | tf_op jit(solution)/shard_map/pallas_call | solution.py:776
  77.1 0.5 slice_bitcast_fusion.2
  77.6 0.6 slice_bitcast_fusion
  78.2 0.6 slice_bitcast_fusion.1
  78.8 0.8 copy.16

commit v4 on v3

--- a/solution.py
+++ b/solution.py
@@ -177,29 +177,18 @@
     lax.fori_loop(1, n2, greet2, 0)
     lax.fori_loop(1, n1, greet1, 0)
 
-    def pack(load, mask_lane, shape):
-        def step(h, both):
-            left, right = both
-            v = load(h)
-            at = 3 * h
-            here = (mask_lane >= at) & (mask_lane < at + 3)
-            left = jnp.where(here, pltpu.roll(v, at, 1), left)
-            right = jnp.where(here, pltpu.roll(v, at + 3, 1), right)
-            return left, right
-
-        zero = jnp.zeros(shape, F32)
-        return lax.fori_loop(0, height, step, (zero, zero))
-
     loads[0].wait()
     for k in range(ch):
         cotf[k * height : (k + 1) * height, :] = cot[k].astype(F32)
 
-    def lift(h, carry):
-        up[h + reach] = cotf[pl.ds(h, ch, stride=height), :]
-        return carry
-
-    lax.fori_loop(0, height, lift, 0)
-    left, right = pack(lambda h: up[h + reach], lane, (ch, lanes))
+    left = jnp.zeros((ch, lanes), F32)
+    right = jnp.zeros((ch, lanes), F32)
+    for h in range(height):
+        v = cotf[pl.ds(h, ch, stride=height), :]
+        up[h + reach] = v
+        here = (lane >= 3 * h) & (lane < 3 * h + 3)
+        left = jnp.where(here, pltpu.roll(v, 3 * h, 1), left)
+        right = jnp.where(here, pltpu.roll(v, 3 * h + 3, 1), right)
     upk[0] = left
     upk[1] = right
     upack[0] = left.astype(BF16)
@@ -339,7 +328,7 @@
     lane16 = lax.broadcasted_iota(jnp.int32, (2 * sub, lanes), 1)
     place3 = lax.rem(lane16, 3)
 
-    def sweep(src, halo, out, flip, first, final):
+    def sweep(src, halo, out, flip, first, final, unroll=1):
         inside = range(tall) if halo is not None else range(reach, height + reach)
 
         def one(step, carry):
@@ -366,7 +355,7 @@
                     out[h, gs] = live.pop(h)
             return carry
 
-        lax.fori_loop(first * side, final * side, one, 0)
+        lax.fori_loop(first * side, final * side, one, 0, unroll=unroll)
 
     def shifted_rows(src, gs, j):
         s = reach - j
@@ -387,7 +376,7 @@
             turns[0, at] = pltpu.roll(pnk[0], (-at) % lanes, 1)
             turns[1, at] = pltpu.roll(pnk[1], (2 - at) % lanes, 1)
 
-    sweep(up, None, ng, True, 0, groups)
+    sweep(up, None, ng, True, 0, groups, 2)
     for copy in u_copies:
         copy.wait_recv()
     for k in range(reach):
@@ -516,38 +505,39 @@
             kgacc[i * side + j, gs] = sumk[i]
         return carry
 
-    lax.fori_loop(0, groups * side, kg_inner, 0)
-
-    for copy in p_copies:
+    lax.fori_loop(0, groups * side, kg_inner, 0, unroll=4)
+
+    for copy in p_copies[:2]:
         copy.wait_recv()
     for k in range(reach):
         ks = slice(k * lanes, (k + 1) * lanes)
         nor[k] = jnp.where(top, finish(embed(prow[0, :, ks])[0]), 0.0)
         nor[height + reach + k] = jnp.where(bottom, finish(embed(prow[1, :, ks])[0]), 0.0)
-    turn(lambda slot: finish(embed(ppeer[slot])[0]))
-
-    def kg_outer(g, carry):
+
+    def kg_rows(g, carry):
         gs = pl.ds(pl.multiple_of(g * 2 * sub, 2 * sub), 2 * sub)
         for j in range(side):
-            s = reach - j
             v = shifted_rows(nor, gs, j)
-            if s > 0:
-                edge = jnp.where(place3 < s, upk[0, gs], 0.0)
-            if s < 0:
-                edge = jnp.where(place3 >= reach + s, upk[1, gs], 0.0)
             for i in range(side):
-                whole = kgacc[i * side + j, gs]
-                for a, tap_row in outer:
-                    if tap_row == i:
-                        whole = whole + up[a - i + reach, gs] * v[a]
-                if s > 0:
-                    whole = whole + edge * turns[0, 3 * i + j, gs]
-                if s < 0:
-                    whole = whole + edge * turns[1, 3 * i + j - 4, gs]
-                kgacc[i * side + j, gs] = whole
-        return carry
-
-    lax.fori_loop(0, ch // (2 * sub), kg_outer, 0)
+                terms = [up[a - i + reach, gs] * v[a] for a, tap_row in outer if tap_row == i]
+                if terms:
+                    kgacc[i * side + j, gs] += functools.reduce(lambda p, q: p + q, terms)
+        return carry
+
+    lax.fori_loop(0, ch // (2 * sub), kg_rows, 0)
+    for copy in p_copies[2:]:
+        copy.wait_recv()
+    turn(lambda slot: finish(embed(ppeer[slot])[0]))
+    spot = lax.rem(lane, 3)
+    for j in range(side):
+        s = reach - j
+        if s:
+            which = 0 if s > 0 else 1
+            edge = jnp.where(spot < s if s > 0 else spot >= reach + s, upk[which], 0.0)
+            for i in range(side):
+                at = 3 * i + j if s > 0 else 3 * i + j - 4
+                kgacc[i * side + j] += edge * turns[which, at]
+
     ones = jnp.ones((lanes, lanes), BF16)
     for at, scale in ((0, 1.0 / factor), (1, 1.0 / factor), (2, 1.0)):
         kgacc[side * side + at] = (sums[at, 0] + sums[at, 1]) * scale

time: 79.7 us -> 78.5 us (0.985)
  Pallas kernels: 76.4 us -> 75.2 us
    pallas_call x1, Pallas kernels: 76.4 us -> 75.2 us  [per_device(): pl.pallas_call(functools.partial(body, place), out_shape=(jax.ShapeDtypeS...]
where the time goes in v4:
time: 78.5 us; the launch traced here: 78.4 us
  Pallas kernels  75.2 us (96%)
  local copies, waits for them, and re-layouts  2.54 us (3%)
    pallas_call x1, Pallas kernels, per_device(): pl.pallas_call(functools.partial(body, place), out_shape=(jax.ShapeDtypeS...  75.2 us

profile of v4, /device:TPU:1, one launch (start us, length us, event | category | flops | bytes accessed | tf_op | source)
XLA Modules:
  0.0 78.4 jit_solution(6181880604302289258)
XLA Ops:
  0.6 75.2 %shard_map.135 = (bf16[64,32,128]{2,1,0:T(8,128)(2,1)S(1)}, f32[128,64]{1,0:T(8,128)S(1)}) custom-call(bf16[48,4096]{1,0:T(8,128)(2,1)} %bitcast.19, bf16[64,32,128]{2,1,0:T(8,128)(2,1)} %cot_in.1, bf16[48,64]{1,0:T(8,128)(2,1)} %bitcast.21, f32[1,64]{1,0:T(1,128)} %bitcast.22, f32[1,64]{1,0:T(1,128)} %bitcast.23, f32[1,64]{1,0:T(1,128)} %bitcast.24, ...), custom_call_target="tpu_custom_call" | custom-call | tf_op jit(solution)/shard_map/pallas_call | solution.py:766
  75.8 0.5 slice_bitcast_fusion.2
  76.4 0.6 slice_bitcast_fusion
  77.0 0.6 slice_bitcast_fusion.1
  77.6 0.8 %copy.16 = bf16[64,32,128]{2,1,0:T(8,128)(2,1)} copy(bf16[64,32,128]{2,1,0:T(8,128)(2,1)S(1)} %get-tuple-element.22) | data formatting | bytes 1048576

commit v5 on v4

--- a/solution.py
+++ b/solution.py
@@ -41,6 +41,8 @@
     up,
     nor,
     norh,
+    xhat,
+    inv,
     ng,
     acc,
     kgacc,
@@ -451,14 +453,8 @@
             right = jnp.where(here, pltpu.roll(v, 3 * h + 3, 1), right)
             hat, deviation = embed(pixels)
             nor[h + reach] = finish(hat)
-            grad = ng[h] * factor
-            sums[0, k] += grad * hat
-            sums[1, k] += grad
-            sums[2, k] += up[h + reach]
-            xgrad = grad * cols[1]
-            mean1 = jnp.mean(xgrad, axis=0, keepdims=True)
-            mean2 = jnp.mean(xgrad * hat, axis=0, keepdims=True)
-            pgb[:, block(h)] = (deviation * (xgrad - mean1 - hat * mean2)).astype(BF16)
+            xhat[h] = hat
+            inv[h] = jnp.broadcast_to(deviation, (sub, lanes))
         return left, right
 
     edges = (jnp.zeros((npix, lanes), F32), jnp.zeros((npix, lanes), F32))
@@ -478,6 +474,21 @@
     for copy in p_copies:
         copy.start()
 
+    def inner_back(pair, carry):
+        for k in range(2):
+            h = 2 * pair + k
+            hat, deviation = xhat[h], inv[h, 0:1]
+            grad = ng[h] * factor
+            sums[0, k] += grad * hat
+            sums[1, k] += grad
+            sums[2, k] += up[h + reach]
+            xgrad = grad * cols[1]
+            mean1 = jnp.mean(xgrad, axis=0, keepdims=True)
+            mean2 = jnp.mean(xgrad * hat, axis=0, keepdims=True)
+            pgb[:, block(h)] = (deviation * (xgrad - mean1 - hat * mean2)).astype(BF16)
+        return carry
+
+    lax.fori_loop(0, height // 2, inner_back, 0)
     grads = lax.dot_general(
         pgb[...], pixb[...], (((1,), (1,)), ((), ())), preferred_element_type=F32
     )
@@ -720,6 +731,8 @@
         pltpu.VMEM((tall,) + plane, F32),
         pltpu.VMEM((tall,) + plane, F32),
         pltpu.VMEM((tall,) + plane, F32),
+        pltpu.VMEM((height,) + plane, F32),
+        pltpu.VMEM((height, sub, lanes), F32),
         pltpu.VMEM((height,) + plane, F32),
         pltpu.VMEM((height,) + plane, F32),
         pltpu.VMEM((side * side + 3,) + plane, F32),

time: 78.5 us -> 78.3 us (level)
  no operation moved by 1% of the time
where the time goes in v5:
time: 78.3 us; the launch traced here: 78.2 us
  Pallas kernels  75 us (96%)
  local copies, waits for them, and re-layouts  2.54 us (3%)
    pallas_call x1, Pallas kernels, per_device(): pl.pallas_call(functools.partial(body, place), out_shape=(jax.ShapeDtypeS...  75 us

profile of v5, /device:TPU:1, one launch (start us, length us, event | category | flops | bytes accessed | tf_op | source)
XLA Modules:
  0.0 78.2 jit_solution(333637291160564015)
XLA Ops:
  0.6 75.0 %shard_map.135 = (bf16[64,32,128]{2,1,0:T(8,128)(2,1)S(1)}, f32[128,64]{1,0:T(8,128)S(1)}) custom-call(bf16[48,4096]{1,0:T(8,128)(2,1)} %bitcast.19, bf16[64,32,128]{2,1,0:T(8,128)(2,1)} %cot_in.1, bf16[48,64]{1,0:T(8,128)(2,1)} %bitcast.21, f32[1,64]{1,0:T(1,128)} %bitcast.22, f32[1,64]{1,0:T(1,128)} %bitcast.23, f32[1,64]{1,0:T(1,128)} %bitcast.24, ...), custom_call_target="tpu_custom_call" | custom-call | tf_op jit(solution)/shard_map/pallas_call | solution.py:779
  75.6 0.5 slice_bitcast_fusion.2
  76.1 0.6 slice_bitcast_fusion
  76.8 0.6 slice_bitcast_fusion.1
  77.4 0.8 %copy.16 = bf16[64,32,128]{2,1,0:T(8,128)(2,1)} copy(bf16[64,32,128]{2,1,0:T(8,128)(2,1)S(1)} %get-tuple-element.22) | data formatting | bytes 1048576
